TPU v7x, 128 devices: a whole 4x4x4 slice. The times are simulated.
128 devices in a mesh: ka: 64 (over y, z_lo, x, core), br: 2 (over z_hi).
Axes of the slice: x: 4, y: 4, z: 4 (z_hi: 2, z_lo: 2; z = z_hi * 2 + z_lo), core: 2. Of those that a mesh axis runs over, the one named last changes fastest.
Arguments:
- occupation: float32 [8, 32768], P(None, 'ka'), may hold values from 0 to 1
- phonons: float32 [12, 4096], P('br', 'ka'), may hold values from 0.05 to 5
- coupling: bfloat16 [16, 12, 8, 8, 32768], P(None, 'br', None, None, 'ka'), may hold values from 0.00049972534 to 0.0079956055
- shifted_point_index: int32 [16, 32768], P(None, 'ka'), may hold values from 0 to 32767
- wavevector_index: int32 [16, 32768], P(None, 'ka'), may hold values from 0 to 4095
- window: int32 [8, 32768], P(None, 'ka'), may hold values 0 or 1
Outputs:
- collision: float32 [8, 32768], P(None, 'ka')
- generation: float32 [12, 4096], P('br', 'ka')
All inputs are finite; a program needn't handle non-finite values. No bound on the sum of `window` on one device may be relied on, other than what follows from the above.
Results may differ from a plain program's by a relative error of at most 0.0003.
Values sent between devices are 32-bit elements; how exact they have to be, the bound alone decides.
No kernel may reach another device: no remote copies, remote signals or barrier semaphores. Data moves between devices by JAX's collectives and lax.ppermute only.
A program may use at most 128 MiB of HBM per device.

v0:
```python
import jax
import jax.numpy as jnp
from jax import lax
from jax.sharding import PartitionSpec as P


def fetch_states(occupation, phonon_share, shifted_point_index):
    collected_values, phonon_full = (
        lax.all_gather(occupation, "ka", axis=1, tiled=True),
        lax.all_gather(phonon_share, "ka", axis=1, tiled=True),
    )
    picked = jnp.take(collected_values, shifted_point_index, axis=1)
    return (jnp.transpose(picked, (1, 0, 2)), phonon_full)


def share_generation(term):
    return lax.psum_scatter(term, "ka", scatter_dimension=1, tiled=True)


def apply_scattering(occupation, beyond_all, phonon_full, coupling, wavevector_index, window):
    window_f = window.astype(jnp.float32)
    num_q = phonon_full.shape[1]

    def slot_step(loop_state, inputs):
        scattering_sum, emission_sum = loop_state
        tile, beyond, q_rows = inputs
        tile = tile.astype(jnp.float32)
        phonon_at = phonon_full[:, q_rows]
        weighted = jnp.einsum("umnk,nk->umk", tile, beyond)
        totals = jnp.sum(tile, axis=2)
        detailed_balance_term = window_f[None] * (
            weighted * (phonon_at[:, None, :] + 1.0)
            - occupation[None] * weighted
            - occupation[None] * totals * phonon_at[:, None, :]
        )
        per_point = jnp.sum(detailed_balance_term, axis=1)
        collected_values = jax.ops.segment_sum(per_point.T, q_rows, num_segments=num_q).T
        return (
            (
                scattering_sum + jnp.sum(detailed_balance_term, axis=0),
                emission_sum + collected_values,
            ),
            None,
        )

    start = (jnp.zeros(occupation.shape, jnp.float32), jnp.zeros(phonon_full.shape, jnp.float32))
    result, _ = lax.scan(slot_step, start, (coupling, beyond_all, wavevector_index))
    collision = lax.psum(result[0], "br")
    return (collision, result[1] / 16.0)


def on_device(occupation, phonons, coupling, shifted_point_index, wavevector_index, window):
    beyond_first, phonon_full = fetch_states(occupation, phonons, shifted_point_index)
    initial_scattering, leading_term = apply_scattering(
        occupation, beyond_first, phonon_full, coupling, wavevector_index, window
    )
    initial_emission = share_generation(leading_term)
    mid_phonons = phonons + 0.1 * initial_emission
    halfway_occupancy = occupation + 0.1 * initial_scattering
    beyond_second, mid_full = fetch_states(halfway_occupancy, mid_phonons, shifted_point_index)
    collision, second_term = apply_scattering(
        halfway_occupancy, beyond_second, mid_full, coupling, wavevector_index, window
    )
    generation = share_generation(second_term)
    return (collision, generation)


def solution(mesh):
    in_specs = (
        P(None, "ka"),
        P("br", "ka"),
        P(None, "br", None, None, "ka"),
        P(None, "ka"),
        P(None, "ka"),
        P(None, "ka"),
    )
    out_specs = (P(None, "ka"), P("br", "ka"))
    return jax.shard_map(
        on_device, mesh=mesh, in_specs=in_specs, out_specs=out_specs, check_vma=False
    )
```

profile of v0, /device:TPU:1, one launch (start us, length us, event | category | flops | bytes accessed | tf_op | source)
XLA Modules:
  0.0 1315.7 jit_solution(5632362504287335286)
XLA Ops:
  10.4 85.7 %all-gather = f32[64,64,6]{1,2,0:T(8,128)S(1)} all-gather(f32[1,64,6]{1,2,0:T(8,128)} %bitcast.157), channel_id=1, replica_groups=mesh['ka'=64,'br'=2] {'ka'}, dimensions={0}, use_global_device_ids=true | all-gather | bytes 99840 | tf_op jit(solution)/shard_map/all_gather | solution.py:10
  98.2 36.9 %all-gather.5.cloned.1.call-done = f32[8,32768]{0,1:T(8,128)} async-done(((f32[8,512]{0,1:T(8,128)}), f32[8,32768]{0,1:T(8,128)}) %all-gather.5.cloned.1.call-update) | async-done | bytes 1048592 | tf_op jit(solution)/shard_map/all_gather | solution.py:9
  135.1 33.4 %gather_fusion.2 = f32[8192,8]{1,0:T(8,128)} fusion(f32[8,32768]{0,1:T(8,128)} %all-gather.5.cloned.1.call-done, s32[8192]{0:T(1024)S(1)} %broadcast_clamp_fusion), kind=kCustom, calls=%fused_computation.clone | custom fusion | bytes 557056 | tf_op jit(solution)/shard_map/jit(_take)/gather | solution.py:12
  168.5 2.8 copy.89
  171.4 193.1 %while.26 = (s32[]{:T(128)}, f32[8,512]{1,0:T(8,128)S(1)}, f32[6,4096]{0,1:T(8,128)}, f32[8,512]{1,0:T(8,128)S(1)}, f32[16,8,512]{2,1,0:T(8,128)S(1)}, /*index=5...) while((s32[]{:T(128)}, f32[8,512]{1,0:T(8,128)S(1)}, ...), condition=%wide.region_5.7_spmd.clone, body=%wide.region_0.6_spmd.clone.sunk | while | flops 1213955 | bytes 1869972 | solution.py:47
  177.6 2.8 scatter_custom_fusion.11
  188.2 2.8 scatter_custom_fusion.11
  191.0 3.2 bitcast_add_fusion.4
  200.4 2.8 scatter_custom_fusion.11
  203.2 3.2 bitcast_add_fusion.4
  212.5 2.8 scatter_custom_fusion.11
  215.3 3.2 bitcast_add_fusion.4
  224.7 2.8 scatter_custom_fusion.11
  227.5 3.2 bitcast_add_fusion.4
  236.9 2.8 scatter_custom_fusion.11
  239.7 3.2 bitcast_add_fusion.4
  249.1 2.8 scatter_custom_fusion.11
  251.8 3.2 bitcast_add_fusion.4
  261.2 2.8 scatter_custom_fusion.11
  264.0 3.2 bitcast_add_fusion.4
  273.4 2.8 scatter_custom_fusion.11
  276.2 3.2 bitcast_add_fusion.4
  285.6 2.8 scatter_custom_fusion.11
  288.3 3.2 bitcast_add_fusion.4
  297.7 2.8 scatter_custom_fusion.11
  300.5 3.2 bitcast_add_fusion.4
  309.9 2.8 scatter_custom_fusion.11
  312.7 3.2 bitcast_add_fusion.4
  322.0 2.8 scatter_custom_fusion.11
  324.8 3.2 bitcast_add_fusion.4
  334.2 2.8 scatter_custom_fusion.11
  337.0 3.2 bitcast_add_fusion.4
  346.4 2.8 scatter_custom_fusion.11
  349.2 3.2 bitcast_add_fusion.4
  358.6 2.8 scatter_custom_fusion.11
  361.3 3.2 bitcast_add_fusion.4
  364.6 13.6 %psum.14 = f32[8,512]{0,1:T(8,128)S(1)} all-reduce(f32[8,512]{0,1:T(8,128)S(1)} %copy.92), channel_id=1, replica_groups=mesh['ka'=64,'br'=2] {'br'}, use_global_device_ids=true, to_apply=%region_6.8 | all-reduce | flops 4096 | bytes 32768 | tf_op jit(solution)/shard_map/psum | solution.py:48
  384.5 280.7 %reduce-scatter.7.cloned.1.call-done = f32[64,6]{1,0:T(8,128)} async-done(((f32[4096,6]{1,0:T(8,128)}), f32[64,6]{1,0:T(8,128)}) %reduce-scatter.7.cloned.1.call-update) | async-done | bytes 1552
  666.0 84.0 %all-gather.1 = f32[64,64,6]{1,2,0:T(8,128)S(1)} all-gather(f32[1,64,6]{1,2,0:T(8,128)S(1)} %add_bitcast_fusion), channel_id=1, replica_groups=mesh['ka'=64,'br'=2] {'ka'}, dimensions={0}, use_global_device_ids=true | all-gather | bytes 99840 | tf_op jit(solution)/shard_map/all_gather | solution.py:10
  752.1 38.7 %all-gather.7.cloned.1.call-done = f32[8,32768]{0,1:T(8,128)} async-done(((f32[8,512]{0,1:T(8,128)}), f32[8,32768]{0,1:T(8,128)}) %all-gather.7.cloned.1.call-update) | async-done | bytes 1048592 | tf_op jit(solution)/shard_map/all_gather | solution.py:9
  790.8 33.4 %gather_fusion.3 = f32[8192,8]{1,0:T(8,128)} fusion(f32[8,32768]{0,1:T(8,128)} %all-gather.7.cloned.1.call-done, s32[8192]{0:T(1024)S(1)} %broadcast_clamp_fusion), kind=kCustom, calls=%fused_computation.3.clone | custom fusion | bytes 557056 | tf_op jit(solution)/shard_map/jit(_take)/gather | solution.py:12
  824.2 2.8 copy.94
  827.1 193.1 %while.27 = (s32[]{:T(128)}, f32[8,512]{1,0:T(8,128)S(1)}, f32[6,4096]{0,1:T(8,128)}, f32[8,512]{1,0:T(8,128)S(1)}, f32[16,8,512]{2,1,0:T(8,128)S(1)}, /*index=5...) while((s32[]{:T(128)}, f32[8,512]{1,0:T(8,128)S(1)}, ...), condition=%wide.region_13.15_spmd.clone, body=%wide.region_8.0_spmd.clone.sunk | while | flops 1213955 | bytes 1869972 | solution.py:47
  843.9 2.8 scatter_custom_fusion.13
  846.7 3.2 bitcast_add_fusion.5
  858.8 3.2 bitcast_add_fusion.5
  871.0 3.2 bitcast_add_fusion.5
  880.4 2.8 scatter_custom_fusion.13
  883.2 3.2 bitcast_add_fusion.5
  895.3 3.2 bitcast_add_fusion.5
  907.5 3.2 bitcast_add_fusion.5
  916.9 2.8 scatter_custom_fusion.13
  919.7 3.2 bitcast_add_fusion.5
  931.8 3.2 bitcast_add_fusion.5
  941.2 2.8 scatter_custom_fusion.13
  944.0 3.2 bitcast_add_fusion.5
  956.2 3.2 bitcast_add_fusion.5
  968.3 3.2 bitcast_add_fusion.5
  980.5 3.2 bitcast_add_fusion.5
  992.7 3.2 bitcast_add_fusion.5
  1004.8 3.2 bitcast_add_fusion.5
  1017.0 3.2 bitcast_add_fusion.5
  1024.4 9.5 psum.15
  1033.9 273.9 %reduce-scatter.9.cloned.1.call-done = f32[64,6]{1,0:T(8,128)} async-done(((f32[4096,6]{1,0:T(8,128)}), f32[64,6]{1,0:T(8,128)}) %reduce-scatter.9.cloned.1.call-update) | async-done | bytes 1552
  (412 shorter events, 255.3 us)
Async XLA Ops:
  7.2 91.0 %copy-start.2 = (s32[16,512]{1,0:T(8,128)S(1)}, s32[16,512]{1,0:T(8,128)}, u32[]{:S(2)}) copy-start(s32[16,512]{1,0:T(8,128)} %param.15) | copy-start | bytes 98308
  7.2 127.9 %all-gather.5.cloned.1.call-start = ((), (), s32[]{:S(2)}) async-start(), calls=%async_computation.2 | async-start | bytes 17039360 | tf_op jit(solution)/shard_map/all_gather | solution.py:9
  8.8 656.3 %reduce-scatter.7.cloned.1.call-start = ((), (), s32[]{:S(2)}) async-start(), calls=%async_computation.4 | async-start | bytes 2129920
  168.5 2.9 copy-start.1
  380.5 2.1 copy-start
  382.5 283.5 %copy-start.3 = (f32[6,64]{1,0:T(8,128)S(1)}, f32[6,64]{1,0:T(8,128)}, u32[]{:S(2)}) copy-start(f32[6,64]{1,0:T(8,128)} %param.13) | copy-start | bytes 4612
  382.5 408.2 %all-gather.7.cloned.1.call-start = ((), (), s32[]{:S(2)}) async-start(), calls=%async_computation.3 | async-start | bytes 17039360 | tf_op jit(solution)/shard_map/all_gather | solution.py:9
  383.4 924.4 %reduce-scatter.9.cloned.1.call-start = ((), (), s32[]{:S(2)}) async-start(), calls=%async_computation.5 | async-start | bytes 2129920
Sparse Core Ops, SparseCore 0:
  9.7 125.3 all-gather.4
  382.7 282.4 reduce-scatter.6
  666.9 123.8 all-gather.6
  1024.5 283.1 reduce-scatter.8
where the time goes:
time: 1330 us; the launch traced here: 1320 us
  waiting for transfers between devices  630 us (47%)
  other arithmetic  295 us (22%)
  blocking collectives  193 us (15%)
  local copies, waits for them, and re-layouts  182 us (14%)
  between operations  13.9 us (1%)
    unnamed x6, waiting for transfers between devices  555 us
    all_gather x2, blocking collectives, fetch_states(): lax.all_gather(phonon_share, 'ka', axis=1, tiled=True)  170 us
    add x32, other arithmetic, slot_step(): emission_sum + collected_values  97.7 us
    scatter-add x32, other arithmetic, slot_step(): jax.ops.segment_sum(per_point.T, q_rows, num_segments=num_q)  88.3 us
    gather x64, local copies, waits for them, and re-layouts, slot_step(): phonon_at = phonon_full[:, q_rows]  87.3 us
    all_gather x2, waiting for transfers between devices, fetch_states(): lax.all_gather(occupation, 'ka', axis=1, tiled=True)  75.6 us
    gather x4, local copies, waits for them, and re-layouts, fetch_states(): picked = jnp.take(collected_values, shifted_point_index, axis=1)  72.5 us
    reduce_sum x32, other arithmetic, slot_step(): totals = jnp.sum(tile, axis=2)  40.7 us
  transfers between devices with their start and end apart: 4, of which 4 were waited for; matrix products, arithmetic and copies ran while one was open for 1% of the time, Pallas kernels for 0%

commit v1 on v0

v1 whole, which is shorter than its diff:
```python
import functools
import jax
import jax.numpy as jnp
from jax import lax
from jax.experimental import pallas as pl
from jax.experimental.pallas import tpu as pltpu
from jax.sharding import Mesh, PartitionSpec as P

F32 = jnp.float32
BF16 = jnp.bfloat16
CHIPS = ("y", "zl", "x")


def split2(a):
    hi = a.astype(BF16)
    return hi, (a - hi.astype(F32)).astype(BF16)


def phase_kernel(
    merge, par_ref, own_ref, oth_ref, f_ref, win_ref, idx_ref, q_ref, g_ref,
    c_ref, gen_ref, t2, p2, x, y, e_s, w_s, v_s, cacc, gacc,
):
    par = par_ref[0]
    for side, ref in enumerate((own_ref, oth_ref)):
        for b in range(2):
            for h in range(2):
                hi, lo = split2(ref[:, (2 * b + h) * 8 : (2 * b + h + 1) * 8, :])
                for part, val in enumerate((hi, lo)):
                    t2[side, :, b, :, part * 256 + h * 128 : part * 256 + (h + 1) * 128] = val
    ph = own_ref[:, 32:40, :]
    if merge:
        ph = ph + oth_ref[:, 32:40, :]
    ph = ph.reshape(16, 2, 8, 128)
    for h in range(2):
        hi, lo = split2(ph[:, h])
        p2[:, :, h * 128 : (h + 1) * 128] = hi
        p2[:, :, 256 + h * 128 : 256 + (h + 1) * 128] = lo
    cacc[...] = jnp.zeros_like(cacc)
    gacc[...] = jnp.zeros_like(gacc)
    t2m = t2.reshape(1024, 512)
    p2m = p2.reshape(128, 512)

    def slot(s, _):
        row = idx_ref[pl.ds(s, 1), :]
        qrow = q_ref[pl.ds(s, 1), :]
        io = lax.broadcasted_iota(jnp.int32, (256, 512), 0)
        oh = jnp.where(io == (row & 255), 1.0, 0.0).astype(BF16)
        ohq = jnp.where(io == (qrow & 255), 1.0, 0.0).astype(BF16)
        x[...] = jnp.dot(t2m[...], jnp.concatenate([oh, oh], axis=0), preferred_element_type=F32)
        y[...] = jnp.dot(p2m[...], jnp.concatenate([ohq, ohq], axis=0), preferred_element_type=F32)
        h = row >> 8
        h = (((h >> 1) & 1) ^ par) * 64 + (h >> 2) * 2 + (h & 1)
        h = jnp.broadcast_to(h, (8, 512))
        acc = [jnp.zeros((8, 512), F32) for _ in range(2)]
        for r in range(128):
            acc[r % 2] = jnp.where(h == r, x[r * 8 : (r + 1) * 8, :], acc[r % 2])
        e_s[...] = acc[0] + acc[1]
        hq = jnp.broadcast_to(qrow >> 8, (8, 512))
        acc = jnp.zeros((8, 512), F32)
        for r in range(16):
            acc = jnp.where(hq == r, y[r * 8 : (r + 1) * 8, :], acc)
        w_s[...] = acc
        for kb in range(4):
            cols = slice(kb * 128, (kb + 1) * 128)
            e = e_s[:, cols]
            d1, d2, ca = [], [], []
            for m in range(8):
                fm = f_ref[m : m + 1, cols]
                wm = win_ref[m : m + 1, cols].astype(F32)
                d1.append((wm * (1.0 - fm)) * e)
                d2.append(wm * (e - fm))
                ca.append(cacc[m, :, cols])
            for u in range(6):
                wu = jnp.broadcast_to(w_s[u : u + 1, cols], (8, 128))
                ga = None
                for m in range(8):
                    tm = g_ref[s, u, m, :, cols].astype(F32) * (d1[m] + wu * d2[m])
                    ca[m] = ca[m] + tm
                    ga = tm if ga is None else ga + tm
                v_s[u : u + 1, cols] = jnp.sum(ga, axis=0, keepdims=True)
            for m in range(8):
                cacc[m, :, cols] = ca[m]
        v = v_s[...]
        v1 = v.astype(BF16).astype(F32)
        r1 = v - v1
        v2 = r1.astype(BF16).astype(F32)
        v3 = r1 - v2
        hm = (lax.broadcasted_iota(jnp.int32, (16, 8, 512), 0)) == (qrow >> 8)[None]
        a = [
            jnp.where(hm, jnp.broadcast_to(vv[None], (16, 8, 512)), 0.0).astype(BF16).reshape(128, 512)
            for vv in (v1, v2, v3)
        ]
        gacc[...] += lax.dot_general(
            jnp.concatenate(a, axis=0), ohq, (((1,), (1,)), ((), ())), preferred_element_type=F32
        )
        return 0

    v_s[...] = jnp.zeros_like(v_s)
    lax.fori_loop(0, 16, slot, 0)
    for m in range(8):
        c_ref[m : m + 1, :] = jnp.sum(cacc[m], axis=0, keepdims=True)
    gs = (gacc[0:128] + gacc[128:256] + gacc[256:384]).reshape(16, 8, 256)
    for h in range(2):
        gen_ref[:, h] = gs[:, :, h * 128 : (h + 1) * 128]


def phase(merge, par, own, oth, f, win, idx, q, g):
    vm = pl.BlockSpec(memory_space=pltpu.VMEM)
    c, gen = pl.pallas_call(
        functools.partial(phase_kernel, merge),
        out_shape=(jax.ShapeDtypeStruct((8, 512), F32), jax.ShapeDtypeStruct((16, 2, 8, 128), F32)),
        in_specs=[pl.BlockSpec(memory_space=pltpu.SMEM)] + [vm] * 7,
        out_specs=(vm, vm),
        scratch_shapes=[
            pltpu.VMEM((2, 32, 2, 8, 512), BF16),
            pltpu.VMEM((16, 8, 512), BF16),
            pltpu.VMEM((1024, 512), F32),
            pltpu.VMEM((128, 512), F32),
            pltpu.VMEM((8, 512), F32),
            pltpu.VMEM((8, 512), F32),
            pltpu.VMEM((8, 512), F32),
            pltpu.VMEM((8, 8, 512), F32),
            pltpu.VMEM((384, 256), F32),
        ],
        name="phase",
    )(par, own, oth, f, win, idx, q, g)
    return c, gen.reshape(32, 8, 128)


def tiles(f):
    return f.reshape(8, 4, 128).transpose(1, 0, 2).reshape(32, 128)


def gather_all(chunk):
    send = jnp.broadcast_to(chunk[None], (32, 40, 128))
    own = lax.all_to_all(send, CHIPS, 0, 0, tiled=True)
    oth = lax.ppermute(own, "c", [(0, 1), (1, 0)])
    return own, oth


def on_device(f, p, g, idx, q, win):
    par = lax.axis_index("c").astype(jnp.int32)
    pt = jnp.pad(jnp.concatenate([p, p], axis=1), ((0, 2), (0, 0)))
    half = (lax.broadcasted_iota(jnp.int32, (8, 128), 1) >> 6) == par
    pt = jnp.where(half, pt, 0.0)
    par1 = par.reshape(1)
    own, oth = gather_all(jnp.concatenate([tiles(f), pt], axis=0))
    pfull = pt + lax.ppermute(pt, "c", [(0, 1), (1, 0)])

    def reduce_gen(gen):
        got = lax.all_to_all(gen, CHIPS, 0, 0, tiled=True)
        got = jnp.sum(got, axis=0)
        return (got + lax.ppermute(got, "c", [(0, 1), (1, 0)])) / 16.0

    def add_br(c):
        return c + lax.ppermute(c, "br", [(0, 1), (1, 0)])

    c1, gen1 = phase(True, par1, own, oth, f, win, idx, q, g)
    gen1 = reduce_gen(gen1)
    f2 = f + 0.1 * add_br(c1)
    p2 = pfull + 0.1 * gen1
    own, oth = gather_all(jnp.concatenate([tiles(f2), p2], axis=0))
    c2, gen2 = phase(False, par1, own, oth, f2, win, idx, q, g)
    gen2 = reduce_gen(gen2)
    gen2 = jnp.where(par == 0, gen2[:6, :64], gen2[:6, 64:])
    return add_br(c2), gen2


def solution(mesh):
    fine = Mesh(mesh.devices.reshape(4, 2, 4, 2, 2), ("y", "zl", "x", "c", "br"))
    ka = ("y", "zl", "x", "c")
    in_specs = (
        P(None, ka), P("br", ka), P(None, "br", None, None, ka), P(None, ka), P(None, ka), P(None, ka),
    )
    out_specs = (P(None, ka), P("br", ka))
    return jax.shard_map(on_device, mesh=fine, in_specs=in_specs, out_specs=out_specs, check_vma=False)
```

time: 1330 us -> 129 us (0.10)
  waiting for transfers between devices: 630 us -> 11 us
  other arithmetic: 295 us -> 4.43 us
  local copies, waits for them, and re-layouts: 182 us -> 1.82 us
  blocking collectives: 193 us -> 34 us
  Pallas kernels: 0 us -> 50.7 us
  starting transfers between devices: 0.16 us -> 25.3 us
    unnamed x6 -> x0, waiting for transfers between devices: 555 us -> none
    all_gather x2 -> x0, blocking collectives: 170 us -> none  [fetch_states(): lax.all_gather(phonon_share, 'ka', axis=1, tiled=True)]
    gather x68 -> x0, local copies, waits for them, and re-layouts: 160 us -> none  [the longest x64 87.3 us: slot_step(): phonon_at = phonon_full[:, q_rows]]
    add x97 -> x3, other arithmetic: 98.8 us -> 2.13 us  [the longest x1 1.33 us: add_br(): return c + lax.ppermute(c, 'br', [(0, 1), (1, 0)])]
    scatter-add x32 -> x0, other arithmetic: 88.3 us -> none  [slot_step(): jax.ops.segment_sum(per_point.T, q_rows, num_segments=num_q)]
    all_gather x2 -> x0, waiting for transfers between devices: 75.6 us -> none  [fetch_states(): lax.all_gather(occupation, 'ka', axis=1, tiled=True)]
    pallas_call x0 -> x2, Pallas kernels: none -> 50.7 us  [phase(): pl.pallas_call(functools.partial(phase_kernel, merge), out_shape=(jax.Sha...]
    reduce_sum x64 -> x2, other arithmetic: 42.7 us -> 0.07 us  [reduce_gen(): got = jnp.sum(got, axis=0)]
  transfers between devices with their start and end apart: 4 -> 9, of which waited for: 4 -> 5; matrix products, arithmetic and copies ran while one was open for 1% -> 2% of each run, Pallas kernels for 0% -> 0%
where the time goes in v1:
time: 129 us; the launch traced here: 128 us
  Pallas kernels  50.7 us (39%)
  blocking collectives  34 us (26%)
  starting transfers between devices  25.3 us (20%)
  waiting for transfers between devices  11 us (9%)
  other arithmetic  4.43 us (3%)
  local copies, waits for them, and re-layouts  1.82 us (1%)
    pallas_call x2, Pallas kernels, phase(): pl.pallas_call(functools.partial(phase_kernel, merge), out_shape=(jax.Sha...  50.7 us
    all_to_all x2, blocking collectives, gather_all(): own = lax.all_to_all(send, CHIPS, 0, 0, tiled=True)  34 us
    all_to_all x2, starting transfers between devices, reduce_gen(): got = lax.all_to_all(gen, CHIPS, 0, 0, tiled=True)  7.73 us
    all_to_all x2, waiting for transfers between devices, reduce_gen(): got = lax.all_to_all(gen, CHIPS, 0, 0, tiled=True)  7.47 us
    ppermute x2, starting transfers between devices, add_br(): return c + lax.ppermute(c, 'br', [(0, 1), (1, 0)])  6.78 us
    ppermute x2, starting transfers between devices, gather_all(): oth = lax.ppermute(own, 'c', [(0, 1), (1, 0)])  6.08 us
    ppermute x2, starting transfers between devices, reduce_gen(): return (got + lax.ppermute(got, 'c', [(0, 1), (1, 0)])) / 16.0  3.76 us
    ppermute x2, waiting for transfers between devices, gather_all(): oth = lax.ppermute(own, 'c', [(0, 1), (1, 0)])  3.45 us
  transfers between devices with their start and end apart: 9, of which 5 were waited for; matrix products, arithmetic and copies ran while one was open for 2% of the time, Pallas kernels for 0%

profile of v1, /device:TPU:1, one launch (start us, length us, event | category | flops | bytes accessed | tf_op | source)
XLA Modules:
  0.0 127.9 jit_solution(8572046808789826303)
XLA Ops:
  0.6 0.0 copy-start.6
  0.6 0.0 copy-start.4
  0.7 0.8 fusion
  1.5 0.7 pad_maximum_fusion
  2.3 20.3 %all_to_all.20.own_ref = f32[32,40,128]{2,1,0:T(8,128)S(1)} all-to-all(f32[32,40,128]{2,1,0:T(8,128)S(1)} %broadcast_in_dim.9), channel_id=1, replica_groups=mesh['y'=4,'zl'=2,'x'=4,'c'=2,'br'=2] {'y','zl','x'}, dimensions={0} | all-to-all | bytes 1310720 | tf_op jit(solution)/shard_map/all_to_all | solution.py:136
  22.5 0.0 copy-start.1
  22.5 2.7 %collective-permute-start = (f32[32,40,128]{2,1,0:T(8,128)S(1)}, f32[32,40,128]{2,1,0:T(8,128)S(1)}, u32[]{:S(2)}, u32[]{:S(2)}) collective-permute-start(f32[32,40,128]{2,1,0:T(8,128)S(1)} %all_to_all.20.own_ref), channel_id=1, source_target_pairs={{0,2},{2,0},{1,3},{3,1},{4,6},{6,4},{5,7},{7,5},{8,10},{10,8},{9,1... | collective-permute-start | bytes 1966088 | tf_op jit(solution)/shard_map/ppermute | solution.py:137
  25.2 1.7 %collective-permute-done.oth_ref = f32[32,40,128]{2,1,0:T(8,128)S(1)} collective-permute-done((f32[32,40,128]{2,1,0:T(8,128)S(1)}, f32[32,40,128]{2,1,0:T(8,128)S(1)}, u32[]{:S(2)}, u32[]{:S(2)}) %collective-permute-start) | collective-permute-done | bytes 655392 | tf_op jit(solution)/shard_map/ppermute | solution.py:137
  27.0 0.0 copy-start.3
  27.0 0.0 copy-done.1
  27.0 0.8 copy-done.3
  27.8 25.3 %phase.2 = (f32[8,512]{1,0:T(8,128)}, f32[16,2,8,128]{3,2,1,0:T(8,128)}) custom-call(s32[1]{0:T(128)} %bitcast.par_ref, f32[32,40,128]{2,1,0:T(8,128)} %copy-done.1, f32[32,40,128]{2,1,0:T(8,128)} %copy-done.3, f32[8,512]{1,0:T(8,128)} %f_ref.1, s32[8,512]{1,0:T(8,128)} %win_ref.3, s32[16,512]{1,0:T(8,128)} %idx_ref.3, s32[16,512]{1,0:T(8,128)} %q_ref.3, ...), custom_call_target="tpu_custom_call" | custom-call | tf_op jit(solution)/shard_map/phase/pallas_call | solution.py:109
  53.1 3.9 %all-to-all-start.1 = ((f32[32,8,128]{2,1,0:T(8,128)}), f32[32,8,128]{2,1,0:T(8,128)S(1)}, u32[]{:S(2)}, u32[]{:S(2)}) async-start(f32[32,8,128]{2,1,0:T(8,128)} %bitcast.15), calls=%async_computation.1 | async-start | bytes 262144 | tf_op jit(solution)/shard_map/all_to_all | solution.py:151
  57.0 3.4 %collective-permute-start.1 = (f32[8,512]{1,0:T(8,128)}, f32[8,512]{1,0:T(8,128)S(1)}, u32[]{:S(2)}, u32[]{:S(2)}) collective-permute-start(f32[8,512]{1,0:T(8,128)} %get-tuple-element.6), channel_id=1, source_target_pairs={{0,1},{1,0},{2,3},{3,2},{4,5},{5,4},{6,7},{7,6},{8,9},{9,8},{10,11... | collective-permute-start | bytes 49160 | tf_op jit(solution)/shard_map/ppermute | solution.py:156
  60.4 0.9 collective-permute-start.2
  61.3 3.3 %all-to-all-done.1 = f32[32,8,128]{2,1,0:T(8,128)S(1)} async-done(((f32[32,8,128]{2,1,0:T(8,128)}), f32[32,8,128]{2,1,0:T(8,128)S(1)}, u32[]{:S(2)}, u32[]{:S(2)}) %all-to-all-start.1) | async-done | bytes 131104 | tf_op jit(solution)/shard_map/all_to_all | solution.py:151
  64.6 1.9 %collective-permute-start.3 = (f32[8,128]{1,0:T(8,128)S(1)}, f32[8,128]{1,0:T(8,128)S(1)}, u32[]{:S(2)}, u32[]{:S(2)}) collective-permute-start(f32[8,128]{1,0:T(8,128)S(1)} %reduce_sum.18), channel_id=1, source_target_pairs={{0,2},{2,0},{1,3},{3,1},{4,6},{6,4},{5,7},{7,5},{8,10},{10,8},{9,1... | collective-permute-start | bytes 12296 | tf_op jit(solution)/shard_map/ppermute | solution.py:153
  66.5 0.0 collective-permute-done.1
  66.5 0.0 copy-done.4
  66.5 0.7 multiply_add_fusion.f_ref
  67.3 0.0 copy-start.5
  67.3 0.0 collective-permute-done.2
  67.3 0.1 collective-permute-done.3
  67.3 0.0 copy-done.6
  67.3 0.1 multiply_add_fusion.1
  67.5 13.8 %all_to_all.21.own_ref = f32[32,40,128]{2,1,0:T(8,128)S(1)} all-to-all(f32[32,40,128]{2,1,0:T(8,128)S(1)} %broadcast_in_dim.18), channel_id=1, replica_groups=mesh['y'=4,'zl'=2,'x'=4,'c'=2,'br'=2] {'y','zl','x'}, dimensions={0} | all-to-all | bytes 1310720 | tf_op jit(solution)/shard_map/all_to_all | solution.py:136
  81.2 0.0 copy-start
  81.2 3.4 %collective-permute-start.4 = (f32[32,40,128]{2,1,0:T(8,128)S(1)}, f32[32,40,128]{2,1,0:T(8,128)S(1)}, u32[]{:S(2)}, u32[]{:S(2)}) collective-permute-start(f32[32,40,128]{2,1,0:T(8,128)S(1)} %all_to_all.21.own_ref), channel_id=1, source_target_pairs={{0,2},{2,0},{1,3},{3,1},{4,6},{6,4},{5,7},{7,5},{8,10},{10,8},{9,1... | collective-permute-start | bytes 1966088 | tf_op jit(solution)/shard_map/ppermute | solution.py:137
  84.6 1.7 %collective-permute-done.4.oth_ref = f32[32,40,128]{2,1,0:T(8,128)S(1)} collective-permute-done((f32[32,40,128]{2,1,0:T(8,128)S(1)}, f32[32,40,128]{2,1,0:T(8,128)S(1)}, u32[]{:S(2)}, u32[]{:S(2)}) %collective-permute-start.4) | collective-permute-done | bytes 655392 | tf_op jit(solution)/shard_map/ppermute | solution.py:137
  86.3 0.0 copy-done.5
  86.3 0.0 copy-done
  86.3 0.0 copy-start.2
  86.4 0.9 copy-done.2
  87.2 25.3 %phase.3 = (f32[8,512]{1,0:T(8,128)}, f32[16,2,8,128]{3,2,1,0:T(8,128)}) custom-call(s32[1]{0:T(128)} %bitcast.par_ref, f32[32,40,128]{2,1,0:T(8,128)} %copy-done, f32[32,40,128]{2,1,0:T(8,128)} %copy-done.2, f32[8,512]{1,0:T(8,128)} %copy-done.5, s32[8,512]{1,0:T(8,128)} %win_ref.3, s32[16,512]{1,0:T(8,128)} %idx_ref.3, s32[16,512]{1,0:T(8,128)} %q_ref.3, ...), custom_call_target="tpu_custom_call" | custom-call | tf_op jit(solution)/shard_map/phase/pallas_call | solution.py:109
  112.5 3.9 %all-to-all-start.3 = ((f32[32,8,128]{2,1,0:T(8,128)}), f32[32,8,128]{2,1,0:T(8,128)S(1)}, u32[]{:S(2)}, u32[]{:S(2)}) async-start(f32[32,8,128]{2,1,0:T(8,128)} %bitcast.16), calls=%async_computation.3 | async-start | bytes 262144 | tf_op jit(solution)/shard_map/all_to_all | solution.py:151
  116.4 3.4 %collective-permute-start.5 = (f32[8,512]{1,0:T(8,128)}, f32[8,512]{1,0:T(8,128)S(1)}, u32[]{:S(2)}, u32[]{:S(2)}) collective-permute-start(f32[8,512]{1,0:T(8,128)} %get-tuple-element.8), channel_id=1, source_target_pairs={{0,1},{1,0},{2,3},{3,2},{4,5},{5,4},{6,7},{7,6},{8,9},{9,8},{10,11... | collective-permute-start | bytes 49160 | tf_op jit(solution)/shard_map/ppermute | solution.py:156
  119.8 4.2 %all-to-all-done.3 = f32[32,8,128]{2,1,0:T(8,128)S(1)} async-done(((f32[32,8,128]{2,1,0:T(8,128)}), f32[32,8,128]{2,1,0:T(8,128)S(1)}, u32[]{:S(2)}, u32[]{:S(2)}) %all-to-all-start.3) | async-done | bytes 131104 | tf_op jit(solution)/shard_map/all_to_all | solution.py:151
  124.0 1.9 %collective-permute-start.6 = (f32[8,128]{1,0:T(8,128)S(1)}, f32[8,128]{1,0:T(8,128)S(1)}, u32[]{:S(2)}, u32[]{:S(2)}) collective-permute-start(f32[8,128]{1,0:T(8,128)S(1)} %reduce_sum.19), channel_id=1, source_target_pairs={{0,2},{2,0},{1,3},{3,1},{4,6},{6,4},{5,7},{7,5},{8,10},{10,8},{9,1... | collective-permute-start | bytes 12296 | tf_op jit(solution)/shard_map/ppermute | solution.py:153
  125.9 0.0 collective-permute-done.5
  125.9 1.3 %add.28 = f32[8,512]{1,0:T(8,128)} add(f32[8,512]{1,0:T(8,128)} %get-tuple-element.8, f32[8,512]{1,0:T(8,128)S(1)} %collective-permute-done.5) | non-fusion elementwise | flops 4096 | bytes 49152 | tf_op jit(solution)/shard_map/add | solution.py:156
  127.3 0.0 collective-permute-done.6
  127.3 0.7 slice_select_fusion
  (7 shorter events, 0.2 us)
Async XLA Ops:
  0.6 66.7 %copy-start.6 = (f32[6,64]{1,0:T(8,128)S(1)}, f32[6,64]{1,0:T(8,128)}, u32[]{:S(2)}) copy-start(f32[6,64]{1,0:T(8,128)} %param.7) | copy-start | bytes 4612
  0.6 65.9 %copy-start.4 = (f32[8,512]{1,0:T(8,128)S(1)}, f32[8,512]{1,0:T(8,128)}, u32[]{:S(2)}) copy-start(f32[8,512]{1,0:T(8,128)} %f_ref.1) | copy-start | bytes 49156
  22.5 4.4 %copy-start.1 = (f32[32,40,128]{2,1,0:T(8,128)}, f32[32,40,128]{2,1,0:T(8,128)S(1)}, u32[]{:S(2)}) copy-start(f32[32,40,128]{2,1,0:T(8,128)S(1)} %all_to_all.20.own_ref) | copy-start | bytes 1966084
  22.5 4.4 %collective-permute-start = (f32[32,40,128]{2,1,0:T(8,128)S(1)}, f32[32,40,128]{2,1,0:T(8,128)S(1)}, u32[]{:S(2)}, u32[]{:S(2)}) collective-permute-start(f32[32,40,128]{2,1,0:T(8,128)S(1)} %all_to_all.20.own_ref), channel_id=1, source_target_pairs={{0,2},{2,0},{1,3},{3,1},{4,6},{6,4},{5,7},{7,5},{8,10},{10,8},{9,1... | collective-permute-start | bytes 1966088 | tf_op jit(solution)/shard_map/ppermute | solution.py:137
  27.0 0.9 copy-start.3
  53.1 11.5 %all-to-all-start.1 = ((f32[32,8,128]{2,1,0:T(8,128)}), f32[32,8,128]{2,1,0:T(8,128)S(1)}, u32[]{:S(2)}, u32[]{:S(2)}) async-start(f32[32,8,128]{2,1,0:T(8,128)} %bitcast.15), calls=%async_computation.1 | async-start | bytes 262144 | tf_op jit(solution)/shard_map/all_to_all | solution.py:151
  57.0 9.5 %collective-permute-start.1 = (f32[8,512]{1,0:T(8,128)}, f32[8,512]{1,0:T(8,128)S(1)}, u32[]{:S(2)}, u32[]{:S(2)}) collective-permute-start(f32[8,512]{1,0:T(8,128)} %get-tuple-element.6), channel_id=1, source_target_pairs={{0,1},{1,0},{2,3},{3,2},{4,5},{5,4},{6,7},{7,6},{8,9},{9,8},{10,11... | collective-permute-start | bytes 49160 | tf_op jit(solution)/shard_map/ppermute | solution.py:156
  60.4 6.9 %collective-permute-start.2 = (f32[8,128]{1,0:T(8,128)S(1)}, f32[8,128]{1,0:T(8,128)S(1)}, u32[]{:S(2)}, u32[]{:S(2)}) collective-permute-start(f32[8,128]{1,0:T(8,128)S(1)} %fusion), channel_id=1, source_target_pairs={{0,2},{2,0},{1,3},{3,1},{4,6},{6,4},{5,7},{7,5},{8,10},{10,8},{9,1... | collective-permute-start | bytes 12296 | tf_op jit(solution)/shard_map/ppermute | solution.py:148
  64.6 2.7 %collective-permute-start.3 = (f32[8,128]{1,0:T(8,128)S(1)}, f32[8,128]{1,0:T(8,128)S(1)}, u32[]{:S(2)}, u32[]{:S(2)}) collective-permute-start(f32[8,128]{1,0:T(8,128)S(1)} %reduce_sum.18), channel_id=1, source_target_pairs={{0,2},{2,0},{1,3},{3,1},{4,6},{6,4},{5,7},{7,5},{8,10},{10,8},{9,1... | collective-permute-start | bytes 12296 | tf_op jit(solution)/shard_map/ppermute | solution.py:153
  67.3 19.1 %copy-start.5 = (f32[8,512]{1,0:T(8,128)}, f32[8,512]{1,0:T(8,128)S(1)}, u32[]{:S(2)}) copy-start(f32[8,512]{1,0:T(8,128)S(1)} %multiply_add_fusion.f_ref) | copy-start | bytes 49156
  81.2 5.1 %copy-start = (f32[32,40,128]{2,1,0:T(8,128)}, f32[32,40,128]{2,1,0:T(8,128)S(1)}, u32[]{:S(2)}) copy-start(f32[32,40,128]{2,1,0:T(8,128)S(1)} %all_to_all.21.own_ref) | copy-start | bytes 1966084
  81.2 5.1 %collective-permute-start.4 = (f32[32,40,128]{2,1,0:T(8,128)S(1)}, f32[32,40,128]{2,1,0:T(8,128)S(1)}, u32[]{:S(2)}, u32[]{:S(2)}) collective-permute-start(f32[32,40,128]{2,1,0:T(8,128)S(1)} %all_to_all.21.own_ref), channel_id=1, source_target_pairs={{0,2},{2,0},{1,3},{3,1},{4,6},{6,4},{5,7},{7,5},{8,10},{10,8},{9,1... | collective-permute-start | bytes 1966088 | tf_op jit(solution)/shard_map/ppermute | solution.py:137
  86.3 0.9 copy-start.2
  112.5 11.5 %all-to-all-start.3 = ((f32[32,8,128]{2,1,0:T(8,128)}), f32[32,8,128]{2,1,0:T(8,128)S(1)}, u32[]{:S(2)}, u32[]{:S(2)}) async-start(f32[32,8,128]{2,1,0:T(8,128)} %bitcast.16), calls=%async_computation.3 | async-start | bytes 262144 | tf_op jit(solution)/shard_map/all_to_all | solution.py:151
  116.4 9.5 %collective-permute-start.5 = (f32[8,512]{1,0:T(8,128)}, f32[8,512]{1,0:T(8,128)S(1)}, u32[]{:S(2)}, u32[]{:S(2)}) collective-permute-start(f32[8,512]{1,0:T(8,128)} %get-tuple-element.8), channel_id=1, source_target_pairs={{0,1},{1,0},{2,3},{3,2},{4,5},{5,4},{6,7},{7,6},{8,9},{9,8},{10,11... | collective-permute-start | bytes 49160 | tf_op jit(solution)/shard_map/ppermute | solution.py:156
  124.0 3.2 %collective-permute-start.6 = (f32[8,128]{1,0:T(8,128)S(1)}, f32[8,128]{1,0:T(8,128)S(1)}, u32[]{:S(2)}, u32[]{:S(2)}) collective-permute-start(f32[8,128]{1,0:T(8,128)S(1)} %reduce_sum.19), channel_id=1, source_target_pairs={{0,2},{2,0},{1,3},{3,1},{4,6},{6,4},{5,7},{7,5},{8,10},{10,8},{9,1... | collective-permute-start | bytes 12296 | tf_op jit(solution)/shard_map/ppermute | solution.py:153

commit v2 on v1

v2 whole, which is shorter than its diff:
```python
import functools
import jax
import jax.numpy as jnp
from jax import lax
from jax.experimental import pallas as pl
from jax.experimental.pallas import tpu as pltpu
from jax.sharding import Mesh, PartitionSpec as P

F32 = jnp.float32
BF16 = jnp.bfloat16
I32 = jnp.int32
CHIPS = ("y", "zl", "x")
SWAP = [(0, 1), (1, 0)]


def split2(a):
    hi = a.astype(BF16)
    return hi, (a - hi.astype(F32)).astype(BF16)


def rows_are(sel, index):
    io = lax.broadcasted_iota(I32, (sel, index.shape[1]), 0)
    return jnp.where(io == index, 1.0, 0.0).astype(BF16)


def table_parts(tab_ref, t2):
    for kb in range(4):
        for part, val in enumerate(split2(tab_ref[:, kb * 8 : (kb + 1) * 8, :])):
            t2[:, part, :, kb * 128 : (kb + 1) * 128] = val


def pick(count, index, x):
    index = jnp.broadcast_to(index, (8, 512))
    hi = jnp.zeros((8, 512), F32)
    lo = jnp.zeros((8, 512), F32)
    for r in range(count):
        hit = index == r
        hi = jnp.where(hit, x[r * 16 : r * 16 + 8, :], hi)
        lo = jnp.where(hit, x[r * 16 + 8 : r * 16 + 16, :], lo)
    return hi + lo


def look_up(t2, x, row, parity):
    lo = jnp.where(((row >> 9) & 1) == parity, row & 511, -1)
    x[...] = jnp.dot(t2.reshape(512, 512)[...], rows_are(512, lo), preferred_element_type=F32)
    return pick(32, row >> 10, x)


def start_kernel(par_ref, f_ref, p_ref, idx_ref, q_ref, win_ref, send_ref, f_out, idx_out, q_out, win_out):
    p = p_ref[...]
    lane = lax.broadcasted_iota(I32, (6, 128), 1)
    p = jnp.where((lane >> 6) == par_ref[0], jnp.concatenate([p, p], axis=1), 0.0)
    for kb in range(4):
        tile = f_ref[:, kb * 128 : (kb + 1) * 128]
        send_ref[:, kb * 8 : (kb + 1) * 8, :] = jnp.broadcast_to(tile[None], (32, 8, 128))
    p = jnp.concatenate([p, jnp.zeros((2, 128), F32)], axis=0)
    send_ref[:, 32:40, :] = jnp.broadcast_to(p[None], (32, 8, 128))
    f_out[...] = f_ref[...]
    idx_out[...] = idx_ref[...]
    q_out[...] = q_ref[...]
    win_out[...] = win_ref[...]


def own_kernel(par_ref, own_ref, idx_ref, e_ref, t2, xa, xb):
    par = par_ref[0]
    table_parts(own_ref, t2)

    def step(i, _):
        for k, x in enumerate((xa, xb)):
            s = i * 2 + k
            e_ref[s] = look_up(t2, x, idx_ref[pl.ds(s, 1), :], par)
        return 0

    lax.fori_loop(0, 8, step, 0)


def main_kernel(
    merge, par_ref, own_ref, oth_ref, e_ref, f_ref, win_ref, idx_ref, q_ref, g_hbm,
    c_ref, gen_ref, g_ref, t2, p2, xa, ya, xb, yb, ea, wa, va, eb, wb, vb, fw, cacc, gacc, sems,
):
    for s in range(16):
        pltpu.make_async_copy(g_hbm.at[s], g_ref.at[s], sems.at[s]).start()
    other = 1 - par_ref[0]
    table_parts(oth_ref, t2)
    ph = own_ref[:, 32:40, :]
    if merge:
        ph = ph + oth_ref[:, 32:40, :]
    ph = ph.reshape(16, 2, 8, 128)
    for h in range(2):
        for part, val in enumerate(split2(ph[:, h])):
            p2[:, part, :, h * 128 : (h + 1) * 128] = val
    for m in range(8):
        fm = jnp.broadcast_to(f_ref[m : m + 1, :], (8, 512))
        wm = jnp.broadcast_to(win_ref[m : m + 1, :].astype(F32), (8, 512))
        fw[0, m] = wm * (1.0 - fm)
        fw[1, m] = wm
        fw[2, m] = fm
    cacc[...] = jnp.zeros_like(cacc)
    gacc[...] = jnp.zeros_like(gacc)
    va[...] = jnp.zeros_like(va)
    vb[...] = jnp.zeros_like(vb)

    def look(s, x, y, e_s, w_s):
        qrow = q_ref[pl.ds(s, 1), :]
        y[...] = jnp.dot(
            p2.reshape(256, 256)[...], rows_are(256, qrow & 255), preferred_element_type=F32
        )
        e_s[...] = look_up(t2, x, idx_ref[pl.ds(s, 1), :], other) + e_ref[s]
        w_s[...] = pick(16, qrow >> 8, y)

    def contract(s, e_s, w_s, v_s):
        pltpu.make_async_copy(g_hbm.at[s], g_ref.at[s], sems.at[s]).wait()
        for kb in range(4):
            cols = slice(kb * 128, (kb + 1) * 128)
            e = e_s[:, cols]
            d1, d2, ca = [], [], []
            for m in range(8):
                d1.append(fw[0, m, :, cols] * e)
                d2.append(fw[1, m, :, cols] * (e - fw[2, m, :, cols]))
                ca.append(cacc[m, :, cols])
            for u in range(6):
                wu = jnp.broadcast_to(w_s[u : u + 1, cols], (8, 128))
                ga = None
                for m in range(8):
                    tm = g_ref[s, u, m, :, cols].astype(F32) * (d1[m] + wu * d2[m])
                    ca[m] = ca[m] + tm
                    ga = tm if ga is None else ga + tm
                v_s[u : u + 1, cols] = jnp.sum(ga, axis=0, keepdims=True)
            for m in range(8):
                cacc[m, :, cols] = ca[m]

    def scatter(s, v_s):
        qrow = q_ref[pl.ds(s, 1), :]
        v = v_s[...]
        v1 = v.astype(BF16).astype(F32)
        v2 = v - v1
        hm = lax.broadcasted_iota(I32, (16, 8, 512), 0) == (qrow >> 8)[None]
        a = [
            jnp.where(hm, jnp.broadcast_to(vv[None], (16, 8, 512)), 0.0).astype(BF16).reshape(128, 512)
            for vv in (v1, v2)
        ]
        gacc[...] += lax.dot_general(
            jnp.concatenate(a, axis=0), rows_are(256, qrow & 255), (((1,), (1,)), ((), ())),
            preferred_element_type=F32,
        )

    look(0, xa, ya, ea, wa)

    def step(i, _):
        s = 2 * i
        look(s + 1, xb, yb, eb, wb)
        scatter(jnp.maximum(s - 1, 0), vb)
        contract(s, ea, wa, va)
        look(jnp.minimum(s + 2, 15), xa, ya, ea, wa)
        scatter(s, va)
        contract(s + 1, eb, wb, vb)
        return 0

    lax.fori_loop(0, 8, step, 0)
    scatter(15, vb)
    for m in range(8):
        c_ref[m : m + 1, :] = jnp.sum(cacc[m], axis=0, keepdims=True)
    gs = (gacc[0:128] + gacc[128:256]).reshape(16, 8, 256)
    for h in range(2):
        gen_ref[:, h] = gs[:, :, h * 128 : (h + 1) * 128]


VM = pl.BlockSpec(memory_space=pltpu.VMEM)
SM = pl.BlockSpec(memory_space=pltpu.SMEM)


def in_vmem(a):
    return pltpu.with_memory_space_constraint(a, pltpu.VMEM)


def in_hbm(a):
    return pltpu.with_memory_space_constraint(a, pltpu.HBM)


def phase(merge, par, own, oth, f, win, idx, q, g):
    scratch = [
        pltpu.VMEM((32, 2, 8, 512), BF16),
        pltpu.VMEM((512, 512), F32),
        pltpu.VMEM((512, 512), F32),
    ]
    own, oth, f, win, idx, q = map(in_vmem, (own, oth, f, win, idx, q))
    g = in_hbm(g)
    e = pl.pallas_call(
        own_kernel,
        out_shape=pltpu.VMEM((16, 8, 512), F32),
        in_specs=[SM, VM, VM],
        out_specs=VM,
        scratch_shapes=scratch,
        compiler_params=pltpu.CompilerParams(vmem_limit_bytes=12 << 20),
        name="own",
    )(par, own, idx)
    c, gen = pl.pallas_call(
        functools.partial(main_kernel, merge),
        out_shape=(pltpu.VMEM((8, 512), F32), pltpu.VMEM((16, 2, 8, 128), F32)),
        in_specs=[SM] + [VM] * 7 + [pl.BlockSpec(memory_space=pltpu.HBM)],
        out_specs=(VM, VM),
        scratch_shapes=[
            pltpu.VMEM((16, 6, 8, 8, 512), BF16),
            pltpu.VMEM((32, 2, 8, 512), BF16),
            pltpu.VMEM((16, 2, 8, 256), BF16),
            *([pltpu.VMEM((512, 512), F32), pltpu.VMEM((256, 512), F32)] * 2),
            *([pltpu.VMEM((8, 512), F32)] * 6),
            pltpu.VMEM((3, 8, 8, 512), F32),
            pltpu.VMEM((8, 8, 512), F32),
            pltpu.VMEM((256, 256), F32),
            pltpu.SemaphoreType.DMA((16,)),
        ],
        compiler_params=pltpu.CompilerParams(vmem_limit_bytes=24 << 20),
        name="main",
    )(par, own, oth, in_vmem(e), f, win, idx, q, g)
    return c, gen.reshape(32, 8, 128)


def tiles(f):
    return f.reshape(8, 4, 128).transpose(1, 0, 2).reshape(32, 128)


def gather_all(send):
    own = lax.all_to_all(send, CHIPS, 0, 0, tiled=True)
    return own, lax.ppermute(own, "c", SWAP)


def on_device(f, p, g, idx, q, win):
    par = lax.axis_index("c").astype(I32)
    par1 = par.reshape(1)
    f, p, idx, q, win = map(in_hbm, (f, p, idx, q, win))
    send, f, idx, q, win = pl.pallas_call(
        start_kernel,
        out_shape=(
            pltpu.VMEM((32, 40, 128), F32), pltpu.VMEM((8, 512), F32), pltpu.VMEM((16, 512), I32),
            pltpu.VMEM((16, 512), I32), pltpu.VMEM((8, 512), I32),
        ),
        in_specs=[SM] + [VM] * 5,
        out_specs=(VM,) * 5,
        compiler_params=pltpu.CompilerParams(vmem_limit_bytes=8 << 20),
        name="start",
    )(par1, f, p, idx, q, win)
    own, oth = gather_all(send)
    pt = send[0, 32:40]
    pfull = pt + lax.ppermute(pt, "c", SWAP)

    def reduce_gen(gen):
        got = lax.all_to_all(gen, CHIPS, 0, 0, tiled=True)
        got = jnp.sum(got, axis=0)
        return (got + lax.ppermute(got, "c", SWAP)) / 16.0

    def add_br(c):
        return c + lax.ppermute(c, "br", SWAP)

    c1, gen1 = phase(True, par1, own, oth, f, win, idx, q, g)
    gen1 = reduce_gen(gen1)
    f2 = f + 0.1 * add_br(c1)
    p2 = pfull + 0.1 * gen1
    chunk = jnp.concatenate([tiles(f2), p2], axis=0)
    own, oth = gather_all(jnp.broadcast_to(chunk[None], (32, 40, 128)))
    c2, gen2 = phase(False, par1, own, oth, f2, win, idx, q, g)
    gen2 = reduce_gen(gen2)
    gen2 = jnp.where(par == 0, gen2[:6, :64], gen2[:6, 64:])
    return add_br(c2), gen2


def solution(mesh):
    fine = Mesh(mesh.devices.reshape(4, 2, 4, 2, 2), ("y", "zl", "x", "c", "br"))
    ka = ("y", "zl", "x", "c")
    in_specs = (
        P(None, ka), P("br", ka), P(None, "br", None, None, ka), P(None, ka), P(None, ka), P(None, ka),
    )
    out_specs = (P(None, ka), P("br", ka))
    return jax.shard_map(on_device, mesh=fine, in_specs=in_specs, out_specs=out_specs, check_vma=False)
```

time: 129 us -> 113 us (0.88)
  Pallas kernels: 50.7 us -> 40.1 us
  starting transfers between devices: 25.3 us -> 20.4 us
  waiting for transfers between devices: 11 us -> 15.2 us
  other arithmetic: 4.43 us -> 1.37 us
  local copies, waits for them, and re-layouts: 1.82 us -> 0.05 us
    pallas_call x2 -> x5, Pallas kernels: 50.7 us -> 40.1 us  [the longest x2 27.3 us: phase(): pl.pallas_call(functools.partial(main_kernel, merge), out_shape=(pltpu.VM...]
    all_to_all x2, waiting for transfers between devices: 7.47 us -> 14.2 us  [reduce_gen(): got = lax.all_to_all(gen, CHIPS, 0, 0, tiled=True)]
    ppermute x7, starting transfers between devices: 17.6 us -> 12.6 us  [the longest x2 4.93 us: gather_all(): return (own, lax.ppermute(own, 'c', SWAP))]
    ppermute x7, waiting for transfers between devices: 3.54 us -> 1.02 us  [the longest x2 1.01 us: reduce_gen(): return (got + lax.ppermute(got, 'c', SWAP)) / 16.0]
    unnamed x14 -> x0, local copies, waits for them, and re-layouts: 1.73 us -> none
  transfers between devices with their start and end apart: 9 -> 9, of which waited for: 5 -> 4; matrix products, arithmetic and copies ran while one was open for 2% -> 1% of each run, Pallas kernels for 0% -> 11%
where the time goes in v2:
time: 113 us
  Pallas kernels  40.1 us (35%)
  blocking collectives  35 us (31%)
  starting transfers between devices  20.4 us (18%)
  waiting for transfers between devices  15.2 us (13%)
  other arithmetic  1.37 us (1%)
    all_to_all x2, blocking collectives, gather_all(): own = lax.all_to_all(send, CHIPS, 0, 0, tiled=True)  35 us
    pallas_call x2, Pallas kernels, phase(): pl.pallas_call(functools.partial(main_kernel, merge), out_shape=(pltpu.VM...  27.3 us
    all_to_all x2, waiting for transfers between devices, reduce_gen(): got = lax.all_to_all(gen, CHIPS, 0, 0, tiled=True)  14.2 us
    pallas_call x2, Pallas kernels, phase(): pl.pallas_call(own_kernel, out_shape=pltpu.VMEM((16, 8, 512), F32), in_sp...  11.9 us
    all_to_all x2, starting transfers between devices, reduce_gen(): got = lax.all_to_all(gen, CHIPS, 0, 0, tiled=True)  7.86 us
    ppermute x2, starting transfers between devices, gather_all(): return (own, lax.ppermute(own, 'c', SWAP))  4.93 us
    ppermute x2, starting transfers between devices, add_br(): return c + lax.ppermute(c, 'br', SWAP)  3.78 us
    ppermute x2, starting transfers between devices, reduce_gen(): return (got + lax.ppermute(got, 'c', SWAP)) / 16.0  3.27 us
  transfers between devices with their start and end apart: 9, of which 4 were waited for; matrix products, arithmetic and copies ran while one was open for 1% of the time, Pallas kernels for 11%

profile of v2, /device:TPU:1, one launch (start us, length us, event | category | flops | bytes accessed | tf_op | source)
XLA Modules:
  0.0 112.9 jit_solution(6395570387925982216)
XLA Ops:
  0.6 0.9 start.1
  1.5 20.3 %all_to_all.20.own_ref = f32[32,40,128]{2,1,0:T(8,128)S(1)} all-to-all(f32[32,40,128]{2,1,0:T(8,128)S(1)} %get-tuple-element.12), channel_id=1, replica_groups=mesh['y'=4,'zl'=2,'x'=4,'c'=2,'br'=2] {'y','zl','x'}, dimensions={0} | all-to-all | bytes 1310720 | tf_op jit(solution)/shard_map/all_to_all | solution.py:224
  21.8 2.7 %collective-permute-start = (f32[32,40,128]{2,1,0:T(8,128)S(1)}, f32[32,40,128]{2,1,0:T(8,128)S(1)}, u32[]{:S(2)}, u32[]{:S(2)}) collective-permute-start(f32[32,40,128]{2,1,0:T(8,128)S(1)} %all_to_all.20.own_ref), channel_id=1, source_target_pairs={{0,2},{2,0},{1,3},{3,1},{4,6},{6,4},{5,7},{7,5},{8,10},{10,8},{9,1... | collective-permute-start | bytes 1966088 | tf_op jit(solution)/shard_map/ppermute | solution.py:225
  24.5 5.9 %own.2.e_ref = f32[16,8,512]{2,1,0:T(8,128)S(1)} custom-call(s32[1]{0:T(128)} %bitcast.par_ref, f32[32,40,128]{2,1,0:T(8,128)S(1)} %all_to_all.20.own_ref, s32[16,512]{1,0:T(8,128)S(1)} %get-tuple-element.13.idx_ref), custom_call_target="tpu_custom_call" | custom-call | tf_op jit(solution)/shard_map/own/pallas_call | solution.py:188
  30.4 0.0 collective-permute-done.oth_ref
  30.5 13.7 %main.2 = (f32[8,512]{1,0:T(8,128)S(1)}, f32[16,2,8,128]{3,2,1,0:T(8,128)}) custom-call(s32[1]{0:T(128)} %bitcast.par_ref, f32[32,40,128]{2,1,0:T(8,128)S(1)} %all_to_all.20.own_ref, f32[32,40,128]{2,1,0:T(8,128)S(1)} %collective-permute-done.oth_ref, f32[16,8,512]{2,1,0:T(8,128)S(1)} %own.2.e_ref, f32[8,512]{1,0:T(8,128)S(1)} %get-tuple-element.11.f_ref, ...), custom_call_target="tpu_custom_call" | custom-call | tf_op jit(solution)/shard_map/main/pallas_call | solution.py:197
  44.1 3.4 %collective-permute-start.1 = (f32[8,512]{1,0:T(8,128)S(1)}, f32[8,512]{1,0:T(8,128)S(1)}, u32[]{:S(2)}, u32[]{:S(2)}) collective-permute-start(f32[8,512]{1,0:T(8,128)S(1)} %get-tuple-element.16), channel_id=1, source_target_pairs={{0,1},{1,0},{2,3},{3,2},{4,5},{5,4},{6,7},{7,6},{8,9},{9,8},{10,11... | collective-permute-start | bytes 49160 | tf_op jit(solution)/shard_map/ppermute | solution.py:253
  47.5 3.9 %all-to-all-start.1 = ((f32[32,8,128]{2,1,0:T(8,128)}), f32[32,8,128]{2,1,0:T(8,128)S(1)}, u32[]{:S(2)}, u32[]{:S(2)}) async-start(f32[32,8,128]{2,1,0:T(8,128)} %bitcast.5), calls=%async_computation.1 | async-start | bytes 262144 | tf_op jit(solution)/shard_map/all_to_all | solution.py:248
  51.4 0.6 collective-permute-start.2
  52.0 7.0 %all-to-all-done.1 = f32[32,8,128]{2,1,0:T(8,128)S(1)} async-done(((f32[32,8,128]{2,1,0:T(8,128)}), f32[32,8,128]{2,1,0:T(8,128)S(1)}, u32[]{:S(2)}, u32[]{:S(2)}) %all-to-all-start.1) | async-done | bytes 131104 | tf_op jit(solution)/shard_map/all_to_all | solution.py:248
  59.0 1.8 %collective-permute-start.3 = (f32[8,128]{1,0:T(8,128)S(1)}, f32[8,128]{1,0:T(8,128)S(1)}, u32[]{:S(2)}, u32[]{:S(2)}) collective-permute-start(f32[8,128]{1,0:T(8,128)S(1)} %reduce_sum.18), channel_id=1, source_target_pairs={{0,2},{2,0},{1,3},{3,1},{4,6},{6,4},{5,7},{7,5},{8,10},{10,8},{9,1... | collective-permute-start | bytes 12296 | tf_op jit(solution)/shard_map/ppermute | solution.py:250
  60.7 0.0 collective-permute-done.1
  60.8 0.0 collective-permute-done.2
  60.8 0.8 collective-permute-done.3
  61.6 14.8 %all_to_all.21.own_ref = f32[32,40,128]{2,1,0:T(8,128)S(1)} all-to-all(f32[32,40,128]{2,1,0:T(8,128)S(1)} %broadcast_in_dim.2), channel_id=1, replica_groups=mesh['y'=4,'zl'=2,'x'=4,'c'=2,'br'=2] {'y','zl','x'}, dimensions={0} | all-to-all | bytes 1310720 | tf_op jit(solution)/shard_map/all_to_all | solution.py:224
  76.4 2.2 %collective-permute-start.4 = (f32[32,40,128]{2,1,0:T(8,128)S(1)}, f32[32,40,128]{2,1,0:T(8,128)S(1)}, u32[]{:S(2)}, u32[]{:S(2)}) collective-permute-start(f32[32,40,128]{2,1,0:T(8,128)S(1)} %all_to_all.21.own_ref), channel_id=1, source_target_pairs={{0,2},{2,0},{1,3},{3,1},{4,6},{6,4},{5,7},{7,5},{8,10},{10,8},{9,1... | collective-permute-start | bytes 1966088 | tf_op jit(solution)/shard_map/ppermute | solution.py:225
  78.6 5.9 %own.3.e_ref = f32[16,8,512]{2,1,0:T(8,128)S(1)} custom-call(s32[1]{0:T(128)} %bitcast.par_ref, f32[32,40,128]{2,1,0:T(8,128)S(1)} %all_to_all.21.own_ref, s32[16,512]{1,0:T(8,128)S(1)} %get-tuple-element.13.idx_ref), custom_call_target="tpu_custom_call" | custom-call | tf_op jit(solution)/shard_map/own/pallas_call | solution.py:188
  84.6 0.0 collective-permute-done.4.oth_ref
  84.6 13.6 %main.3 = (f32[8,512]{1,0:T(8,128)S(1)}, f32[16,2,8,128]{3,2,1,0:T(8,128)}) custom-call(s32[1]{0:T(128)} %bitcast.par_ref, f32[32,40,128]{2,1,0:T(8,128)S(1)} %all_to_all.21.own_ref, f32[32,40,128]{2,1,0:T(8,128)S(1)} %collective-permute-done.4.oth_ref, f32[16,8,512]{2,1,0:T(8,128)S(1)} %own.3.e_ref, f32[8,512]{1,0:T(8,128)S(1)} %multiply_add_fusion.f_ref, ...), custom_call_target="tpu_custom_call" | custom-call | tf_op jit(solution)/shard_map/main/pallas_call | solution.py:197
  98.3 4.0 %all-to-all-start.3 = ((f32[32,8,128]{2,1,0:T(8,128)}), f32[32,8,128]{2,1,0:T(8,128)S(1)}, u32[]{:S(2)}, u32[]{:S(2)}) async-start(f32[32,8,128]{2,1,0:T(8,128)} %bitcast.6), calls=%async_computation.3 | async-start | bytes 262144 | tf_op jit(solution)/shard_map/all_to_all | solution.py:248
  102.3 0.4 collective-permute-start.5
  102.7 7.2 %all-to-all-done.3 = f32[32,8,128]{2,1,0:T(8,128)S(1)} async-done(((f32[32,8,128]{2,1,0:T(8,128)}), f32[32,8,128]{2,1,0:T(8,128)S(1)}, u32[]{:S(2)}, u32[]{:S(2)}) %all-to-all-start.3) | async-done | bytes 131104 | tf_op jit(solution)/shard_map/all_to_all | solution.py:248
  109.9 1.5 %collective-permute-start.6 = (f32[8,128]{1,0:T(8,128)S(1)}, f32[8,128]{1,0:T(8,128)S(1)}, u32[]{:S(2)}, u32[]{:S(2)}) collective-permute-start(f32[8,128]{1,0:T(8,128)S(1)} %reduce_sum.19), channel_id=1, source_target_pairs={{0,2},{2,0},{1,3},{3,1},{4,6},{6,4},{5,7},{7,5},{8,10},{10,8},{9,1... | collective-permute-start | bytes 12296 | tf_op jit(solution)/shard_map/ppermute | solution.py:250
  111.4 0.0 collective-permute-done.5
  111.4 0.6 add.26
  112.0 0.2 collective-permute-done.6
  112.2 0.7 slice_select_fusion
  (8 shorter events, 0.1 us)
Async XLA Ops:
  21.8 8.7 %collective-permute-start = (f32[32,40,128]{2,1,0:T(8,128)S(1)}, f32[32,40,128]{2,1,0:T(8,128)S(1)}, u32[]{:S(2)}, u32[]{:S(2)}) collective-permute-start(f32[32,40,128]{2,1,0:T(8,128)S(1)} %all_to_all.20.own_ref), channel_id=1, source_target_pairs={{0,2},{2,0},{1,3},{3,1},{4,6},{6,4},{5,7},{7,5},{8,10},{10,8},{9,1... | collective-permute-start | bytes 1966088 | tf_op jit(solution)/shard_map/ppermute | solution.py:225
  44.1 16.6 %collective-permute-start.1 = (f32[8,512]{1,0:T(8,128)S(1)}, f32[8,512]{1,0:T(8,128)S(1)}, u32[]{:S(2)}, u32[]{:S(2)}) collective-permute-start(f32[8,512]{1,0:T(8,128)S(1)} %get-tuple-element.16), channel_id=1, source_target_pairs={{0,1},{1,0},{2,3},{3,2},{4,5},{5,4},{6,7},{7,6},{8,9},{9,8},{10,11... | collective-permute-start | bytes 49160 | tf_op jit(solution)/shard_map/ppermute | solution.py:253
  47.5 11.5 %all-to-all-start.1 = ((f32[32,8,128]{2,1,0:T(8,128)}), f32[32,8,128]{2,1,0:T(8,128)S(1)}, u32[]{:S(2)}, u32[]{:S(2)}) async-start(f32[32,8,128]{2,1,0:T(8,128)} %bitcast.5), calls=%async_computation.1 | async-start | bytes 262144 | tf_op jit(solution)/shard_map/all_to_all | solution.py:248
  51.4 9.4 %collective-permute-start.2 = (f32[8,128]{1,0:T(8,128)S(1)}, f32[8,128]{1,0:T(8,128)S(1)}, u32[]{:S(2)}, u32[]{:S(2)}) collective-permute-start(f32[8,128]{1,0:T(8,128)S(1)} %slice_bitcast_fusion), channel_id=1, source_target_pairs={{0,2},{2,0},{1,3},{3,1},{4,6},{6,4},{5,7},{7,5},{8,10},{10,8},{9,1... | collective-permute-start | bytes 12296 | tf_op jit(solution)/shard_map/ppermute | solution.py:245
  59.0 2.6 %collective-permute-start.3 = (f32[8,128]{1,0:T(8,128)S(1)}, f32[8,128]{1,0:T(8,128)S(1)}, u32[]{:S(2)}, u32[]{:S(2)}) collective-permute-start(f32[8,128]{1,0:T(8,128)S(1)} %reduce_sum.18), channel_id=1, source_target_pairs={{0,2},{2,0},{1,3},{3,1},{4,6},{6,4},{5,7},{7,5},{8,10},{10,8},{9,1... | collective-permute-start | bytes 12296 | tf_op jit(solution)/shard_map/ppermute | solution.py:250
  76.4 8.2 %collective-permute-start.4 = (f32[32,40,128]{2,1,0:T(8,128)S(1)}, f32[32,40,128]{2,1,0:T(8,128)S(1)}, u32[]{:S(2)}, u32[]{:S(2)}) collective-permute-start(f32[32,40,128]{2,1,0:T(8,128)S(1)} %all_to_all.21.own_ref), channel_id=1, source_target_pairs={{0,2},{2,0},{1,3},{3,1},{4,6},{6,4},{5,7},{7,5},{8,10},{10,8},{9,1... | collective-permute-start | bytes 1966088 | tf_op jit(solution)/shard_map/ppermute | solution.py:225
  98.3 11.6 %all-to-all-start.3 = ((f32[32,8,128]{2,1,0:T(8,128)}), f32[32,8,128]{2,1,0:T(8,128)S(1)}, u32[]{:S(2)}, u32[]{:S(2)}) async-start(f32[32,8,128]{2,1,0:T(8,128)} %bitcast.6), calls=%async_computation.3 | async-start | bytes 262144 | tf_op jit(solution)/shard_map/all_to_all | solution.py:248
  102.3 9.1 %collective-permute-start.5 = (f32[8,512]{1,0:T(8,128)S(1)}, f32[8,512]{1,0:T(8,128)S(1)}, u32[]{:S(2)}, u32[]{:S(2)}) collective-permute-start(f32[8,512]{1,0:T(8,128)S(1)} %get-tuple-element.18), channel_id=1, source_target_pairs={{0,1},{1,0},{2,3},{3,2},{4,5},{5,4},{6,7},{7,6},{8,9},{9,8},{10,11... | collective-permute-start | bytes 49160 | tf_op jit(solution)/shard_map/ppermute | solution.py:253
  109.9 2.3 %collective-permute-start.6 = (f32[8,128]{1,0:T(8,128)S(1)}, f32[8,128]{1,0:T(8,128)S(1)}, u32[]{:S(2)}, u32[]{:S(2)}) collective-permute-start(f32[8,128]{1,0:T(8,128)S(1)} %reduce_sum.19), channel_id=1, source_target_pairs={{0,2},{2,0},{1,3},{3,1},{4,6},{6,4},{5,7},{7,5},{8,10},{10,8},{9,1... | collective-permute-start | bytes 12296 | tf_op jit(solution)/shard_map/ppermute | solution.py:250

commit v3 on v2

--- a/solution.py
+++ b/solution.py
@@ -5,6 +5,7 @@
 from jax.experimental import pallas as pl
 from jax.experimental.pallas import tpu as pltpu
 from jax.sharding import Mesh, PartitionSpec as P
+
 
 F32 = jnp.float32
 BF16 = jnp.bfloat16
@@ -49,7 +50,7 @@
 def start_kernel(par_ref, f_ref, p_ref, idx_ref, q_ref, win_ref, send_ref, f_out, idx_out, q_out, win_out):
     p = p_ref[...]
     lane = lax.broadcasted_iota(I32, (6, 128), 1)
-    p = jnp.where((lane >> 6) == par_ref[0], jnp.concatenate([p, p], axis=1), 0.0)
+    p = jnp.where((lane >> 6) == (par_ref[0] & 1), jnp.concatenate([p, p], axis=1), 0.0)
     for kb in range(4):
         tile = f_ref[:, kb * 128 : (kb + 1) * 128]
         send_ref[:, kb * 8 : (kb + 1) * 8, :] = jnp.broadcast_to(tile[None], (32, 8, 128))
@@ -62,7 +63,7 @@
 
 
 def own_kernel(par_ref, own_ref, idx_ref, e_ref, t2, xa, xb):
-    par = par_ref[0]
+    par = par_ref[0] & 1
     table_parts(own_ref, t2)
 
     def step(i, _):
@@ -76,15 +77,19 @@
 
 def main_kernel(
     merge, par_ref, own_ref, oth_ref, e_ref, f_ref, win_ref, idx_ref, q_ref, g_hbm,
-    c_ref, gen_ref, g_ref, t2, p2, xa, ya, xb, yb, ea, wa, va, eb, wb, vb, fw, cacc, gacc, sems,
+    c_ref, gen_ref, pc_ref, g_ref, t2, p2, xa, ya, xb, yb, ea, wa, va, eb, wb, vb, fw, cacc, gacc, sems,
 ):
     for s in range(16):
         pltpu.make_async_copy(g_hbm.at[s], g_ref.at[s], sems.at[s]).start()
-    other = 1 - par_ref[0]
+    other = 1 - (par_ref[0] & 1)
     table_parts(oth_ref, t2)
     ph = own_ref[:, 32:40, :]
     if merge:
         ph = ph + oth_ref[:, 32:40, :]
+    pc = own_ref[par_ref[0] >> 1, 32:40, :]
+    if merge:
+        pc = pc + oth_ref[par_ref[0] >> 1, 32:40, :]
+    pc_ref[...] = pc
     ph = ph.reshape(16, 2, 8, 128)
     for h in range(2):
         for part, val in enumerate(split2(ph[:, h])):
@@ -194,11 +199,11 @@
         compiler_params=pltpu.CompilerParams(vmem_limit_bytes=12 << 20),
         name="own",
     )(par, own, idx)
-    c, gen = pl.pallas_call(
+    c, gen, pc = pl.pallas_call(
         functools.partial(main_kernel, merge),
-        out_shape=(pltpu.VMEM((8, 512), F32), pltpu.VMEM((16, 2, 8, 128), F32)),
+        out_shape=(pltpu.VMEM((8, 512), F32), pltpu.VMEM((16, 2, 8, 128), F32), pltpu.VMEM((8, 128), F32)),
         in_specs=[SM] + [VM] * 7 + [pl.BlockSpec(memory_space=pltpu.HBM)],
-        out_specs=(VM, VM),
+        out_specs=(VM, VM, VM),
         scratch_shapes=[
             pltpu.VMEM((16, 6, 8, 8, 512), BF16),
             pltpu.VMEM((32, 2, 8, 512), BF16),
@@ -213,7 +218,7 @@
         compiler_params=pltpu.CompilerParams(vmem_limit_bytes=24 << 20),
         name="main",
     )(par, own, oth, in_vmem(e), f, win, idx, q, g)
-    return c, gen.reshape(32, 8, 128)
+    return c, gen.reshape(32, 8, 128), pc
 
 
 def tiles(f):
@@ -227,7 +232,8 @@
 
 def on_device(f, p, g, idx, q, win):
     par = lax.axis_index("c").astype(I32)
-    par1 = par.reshape(1)
+    chip = (lax.axis_index("y") * 2 + lax.axis_index("zl")) * 4 + lax.axis_index("x")
+    par1 = (chip.astype(I32) * 2 + par).reshape(1)
     f, p, idx, q, win = map(in_hbm, (f, p, idx, q, win))
     send, f, idx, q, win = pl.pallas_call(
         start_kernel,
@@ -241,8 +247,6 @@
         name="start",
     )(par1, f, p, idx, q, win)
     own, oth = gather_all(send)
-    pt = send[0, 32:40]
-    pfull = pt + lax.ppermute(pt, "c", SWAP)
 
     def reduce_gen(gen):
         got = lax.all_to_all(gen, CHIPS, 0, 0, tiled=True)
@@ -250,15 +254,16 @@
         return (got + lax.ppermute(got, "c", SWAP)) / 16.0
 
     def add_br(c):
-        return c + lax.ppermute(c, "br", SWAP)
-
-    c1, gen1 = phase(True, par1, own, oth, f, win, idx, q, g)
+        other = lax.ppermute(c, "br", SWAP)
+        return c + other
+
+    c1, gen1, pc = phase(True, par1, own, oth, f, win, idx, q, g)
     gen1 = reduce_gen(gen1)
     f2 = f + 0.1 * add_br(c1)
-    p2 = pfull + 0.1 * gen1
+    p2 = pc + 0.1 * gen1
     chunk = jnp.concatenate([tiles(f2), p2], axis=0)
     own, oth = gather_all(jnp.broadcast_to(chunk[None], (32, 40, 128)))
-    c2, gen2 = phase(False, par1, own, oth, f2, win, idx, q, g)
+    c2, gen2, _ = phase(False, par1, own, oth, f2, win, idx, q, g)
     gen2 = reduce_gen(gen2)
     gen2 = jnp.where(par == 0, gen2[:6, :64], gen2[:6, 64:])
     return add_br(c2), gen2

time: 113 us -> 110 us (0.973)
  waiting for transfers between devices: 15.2 us -> 9.45 us
  starting transfers between devices: 20.4 us -> 22.9 us
    all_to_all x2, waiting for transfers between devices: 14.2 us -> 8.42 us  [reduce_gen(): got = lax.all_to_all(gen, CHIPS, 0, 0, tiled=True)]
    ppermute x3 -> x2, starting transfers between devices: 4.39 us -> 6.77 us  [add_br(): other = lax.ppermute(c, 'br', SWAP)]
  transfers between devices with their start and end apart: 9 -> 8, of which waited for: 4 -> 4; matrix products, arithmetic and copies ran while one was open for 1% -> 1% of each run, Pallas kernels for 11% -> 11%
where the time goes in v3:
time: 110 us; the launch traced here: 109 us
  Pallas kernels  40.1 us (36%)
  blocking collectives  34.7 us (32%)
  starting transfers between devices  22.9 us (21%)
  waiting for transfers between devices  9.45 us (9%)
  other arithmetic  1.37 us (1%)
    all_to_all x2, blocking collectives, gather_all(): own = lax.all_to_all(send, CHIPS, 0, 0, tiled=True)  34.7 us
    pallas_call x2, Pallas kernels, phase(): pl.pallas_call(functools.partial(main_kernel, merge), out_shape=(pltpu.VM...  27.4 us
    pallas_call x2, Pallas kernels, phase(): pl.pallas_call(own_kernel, out_shape=pltpu.VMEM((16, 8, 512), F32), in_sp...  11.9 us
    all_to_all x2, waiting for transfers between devices, reduce_gen(): got = lax.all_to_all(gen, CHIPS, 0, 0, tiled=True)  8.42 us
    all_to_all x2, starting transfers between devices, reduce_gen(): got = lax.all_to_all(gen, CHIPS, 0, 0, tiled=True)  7.76 us
    ppermute x2, starting transfers between devices, add_br(): other = lax.ppermute(c, 'br', SWAP)  6.77 us
    ppermute x2, starting transfers between devices, gather_all(): return (own, lax.ppermute(own, 'c', SWAP))  5.38 us
    ppermute x2, starting transfers between devices, reduce_gen(): return (got + lax.ppermute(got, 'c', SWAP)) / 16.0  3 us
  transfers between devices with their start and end apart: 8, of which 4 were waited for; matrix products, arithmetic and copies ran while one was open for 1% of the time, Pallas kernels for 11%

profile of v3, /device:TPU:1, one launch (start us, length us, event | category | flops | bytes accessed | tf_op | source)
XLA Modules:
  0.0 109.3 jit_solution(13002607082480506521)
XLA Ops:
  0.6 0.9 start.1
  1.5 20.3 %all_to_all.20.own_ref = f32[32,40,128]{2,1,0:T(8,128)S(1)} all-to-all(f32[32,40,128]{2,1,0:T(8,128)S(1)} %get-tuple-element.13), channel_id=1, replica_groups=mesh['y'=4,'zl'=2,'x'=4,'c'=2,'br'=2] {'y','zl','x'}, dimensions={0} | all-to-all | bytes 1310720 | tf_op jit(solution)/shard_map/all_to_all | solution.py:229
  21.8 2.7 %collective-permute-start = (f32[32,40,128]{2,1,0:T(8,128)S(1)}, f32[32,40,128]{2,1,0:T(8,128)S(1)}, u32[]{:S(2)}, u32[]{:S(2)}) collective-permute-start(f32[32,40,128]{2,1,0:T(8,128)S(1)} %all_to_all.20.own_ref), channel_id=1, source_target_pairs={{0,2},{2,0},{1,3},{3,1},{4,6},{6,4},{5,7},{7,5},{8,10},{10,8},{9,1... | collective-permute-start | bytes 1966088 | tf_op jit(solution)/shard_map/ppermute | solution.py:230
  24.5 5.9 %own.2.e_ref = f32[16,8,512]{2,1,0:T(8,128)S(1)} custom-call(s32[1]{0:T(128)} %bitcast.par_ref, f32[32,40,128]{2,1,0:T(8,128)S(1)} %all_to_all.20.own_ref, s32[16,512]{1,0:T(8,128)S(1)} %get-tuple-element.14.idx_ref), custom_call_target="tpu_custom_call" | custom-call | tf_op jit(solution)/shard_map/own/pallas_call | solution.py:193
  30.4 0.0 collective-permute-done.oth_ref
  30.5 13.7 %main.2 = (f32[8,512]{1,0:T(8,128)S(1)}, f32[16,2,8,128]{3,2,1,0:T(8,128)}, f32[8,128]{1,0:T(8,128)S(1)}) custom-call(s32[1]{0:T(128)} %bitcast.par_ref, f32[32,40,128]{2,1,0:T(8,128)S(1)} %all_to_all.20.own_ref, f32[32,40,128]{2,1,0:T(8,128)S(1)} %collective-permute-done.oth_ref, f32[16,8,512]{2,1,0:T(8,128)S(1)} %own.2.e_ref, ...), custom_call_target="tpu_custom_call" | custom-call | tf_op jit(solution)/shard_map/main/pallas_call | solution.py:202
  44.1 3.9 %all-to-all-start.1 = ((f32[32,8,128]{2,1,0:T(8,128)}), f32[32,8,128]{2,1,0:T(8,128)S(1)}, u32[]{:S(2)}, u32[]{:S(2)}) async-start(f32[32,8,128]{2,1,0:T(8,128)} %bitcast.4), calls=%async_computation.1 | async-start | bytes 262144 | tf_op jit(solution)/shard_map/all_to_all | solution.py:252
  48.0 3.4 %collective-permute-start.1 = (f32[8,512]{1,0:T(8,128)S(1)}, f32[8,512]{1,0:T(8,128)S(1)}, u32[]{:S(2)}, u32[]{:S(2)}) collective-permute-start(f32[8,512]{1,0:T(8,128)S(1)} %get-tuple-element.17), channel_id=1, source_target_pairs={{0,1},{1,0},{2,3},{3,2},{4,5},{5,4},{6,7},{7,6},{8,9},{9,8},{10,11... | collective-permute-start | bytes 49160 | tf_op jit(solution)/shard_map/ppermute | solution.py:257
  51.4 4.2 %all-to-all-done.1 = f32[32,8,128]{2,1,0:T(8,128)S(1)} async-done(((f32[32,8,128]{2,1,0:T(8,128)}), f32[32,8,128]{2,1,0:T(8,128)S(1)}, u32[]{:S(2)}, u32[]{:S(2)}) %all-to-all-start.1) | async-done | bytes 131104 | tf_op jit(solution)/shard_map/all_to_all | solution.py:252
  55.7 1.5 %collective-permute-start.2 = (f32[8,128]{1,0:T(8,128)S(1)}, f32[8,128]{1,0:T(8,128)S(1)}, u32[]{:S(2)}, u32[]{:S(2)}) collective-permute-start(f32[8,128]{1,0:T(8,128)S(1)} %reduce_sum.18), channel_id=1, source_target_pairs={{0,2},{2,0},{1,3},{3,1},{4,6},{6,4},{5,7},{7,5},{8,10},{10,8},{9,1... | collective-permute-start | bytes 12296 | tf_op jit(solution)/shard_map/ppermute | solution.py:254
  57.2 0.0 collective-permute-done.1
  57.2 0.8 collective-permute-done.2
  58.0 14.5 %all_to_all.21.own_ref = f32[32,40,128]{2,1,0:T(8,128)S(1)} all-to-all(f32[32,40,128]{2,1,0:T(8,128)S(1)} %broadcast_in_dim.2), channel_id=1, replica_groups=mesh['y'=4,'zl'=2,'x'=4,'c'=2,'br'=2] {'y','zl','x'}, dimensions={0} | all-to-all | bytes 1310720 | tf_op jit(solution)/shard_map/all_to_all | solution.py:229
  72.5 2.7 %collective-permute-start.3 = (f32[32,40,128]{2,1,0:T(8,128)S(1)}, f32[32,40,128]{2,1,0:T(8,128)S(1)}, u32[]{:S(2)}, u32[]{:S(2)}) collective-permute-start(f32[32,40,128]{2,1,0:T(8,128)S(1)} %all_to_all.21.own_ref), channel_id=1, source_target_pairs={{0,2},{2,0},{1,3},{3,1},{4,6},{6,4},{5,7},{7,5},{8,10},{10,8},{9,1... | collective-permute-start | bytes 1966088 | tf_op jit(solution)/shard_map/ppermute | solution.py:230
  75.2 5.9 %own.3.e_ref = f32[16,8,512]{2,1,0:T(8,128)S(1)} custom-call(s32[1]{0:T(128)} %bitcast.par_ref, f32[32,40,128]{2,1,0:T(8,128)S(1)} %all_to_all.21.own_ref, s32[16,512]{1,0:T(8,128)S(1)} %get-tuple-element.14.idx_ref), custom_call_target="tpu_custom_call" | custom-call | tf_op jit(solution)/shard_map/own/pallas_call | solution.py:193
  81.1 0.0 collective-permute-done.3.oth_ref
  81.1 13.7 %main.3 = (f32[8,512]{1,0:T(8,128)S(1)}, f32[16,2,8,128]{3,2,1,0:T(8,128)}, f32[8,128]{1,0:T(8,128)}) custom-call(s32[1]{0:T(128)} %bitcast.par_ref, f32[32,40,128]{2,1,0:T(8,128)S(1)} %all_to_all.21.own_ref, f32[32,40,128]{2,1,0:T(8,128)S(1)} %collective-permute-done.3.oth_ref, f32[16,8,512]{2,1,0:T(8,128)S(1)} %own.3.e_ref, ...), custom_call_target="tpu_custom_call" | custom-call | tf_op jit(solution)/shard_map/main/pallas_call | solution.py:202
  94.8 3.9 %all-to-all-start.3 = ((f32[32,8,128]{2,1,0:T(8,128)}), f32[32,8,128]{2,1,0:T(8,128)S(1)}, u32[]{:S(2)}, u32[]{:S(2)}) async-start(f32[32,8,128]{2,1,0:T(8,128)} %bitcast.5), calls=%async_computation.3 | async-start | bytes 262144 | tf_op jit(solution)/shard_map/all_to_all | solution.py:252
  98.7 3.4 %collective-permute-start.4 = (f32[8,512]{1,0:T(8,128)S(1)}, f32[8,512]{1,0:T(8,128)S(1)}, u32[]{:S(2)}, u32[]{:S(2)}) collective-permute-start(f32[8,512]{1,0:T(8,128)S(1)} %get-tuple-element.20), channel_id=1, source_target_pairs={{0,1},{1,0},{2,3},{3,2},{4,5},{5,4},{6,7},{7,6},{8,9},{9,8},{10,11... | collective-permute-start | bytes 49160 | tf_op jit(solution)/shard_map/ppermute | solution.py:257
  102.1 4.2 %all-to-all-done.3 = f32[32,8,128]{2,1,0:T(8,128)S(1)} async-done(((f32[32,8,128]{2,1,0:T(8,128)}), f32[32,8,128]{2,1,0:T(8,128)S(1)}, u32[]{:S(2)}, u32[]{:S(2)}) %all-to-all-start.3) | async-done | bytes 131104 | tf_op jit(solution)/shard_map/all_to_all | solution.py:252
  106.3 1.5 %collective-permute-start.5 = (f32[8,128]{1,0:T(8,128)S(1)}, f32[8,128]{1,0:T(8,128)S(1)}, u32[]{:S(2)}, u32[]{:S(2)}) collective-permute-start(f32[8,128]{1,0:T(8,128)S(1)} %reduce_sum.19), channel_id=1, source_target_pairs={{0,2},{2,0},{1,3},{3,1},{4,6},{6,4},{5,7},{7,5},{8,10},{10,8},{9,1... | collective-permute-start | bytes 12296 | tf_op jit(solution)/shard_map/ppermute | solution.py:254
  107.8 0.0 collective-permute-done.4
  107.8 0.6 add.34
  108.5 0.2 collective-permute-done.5
  108.7 0.7 slice_select_fusion
  (7 shorter events, 0.1 us)
Async XLA Ops:
  21.8 8.7 %collective-permute-start = (f32[32,40,128]{2,1,0:T(8,128)S(1)}, f32[32,40,128]{2,1,0:T(8,128)S(1)}, u32[]{:S(2)}, u32[]{:S(2)}) collective-permute-start(f32[32,40,128]{2,1,0:T(8,128)S(1)} %all_to_all.20.own_ref), channel_id=1, source_target_pairs={{0,2},{2,0},{1,3},{3,1},{4,6},{6,4},{5,7},{7,5},{8,10},{10,8},{9,1... | collective-permute-start | bytes 1966088 | tf_op jit(solution)/shard_map/ppermute | solution.py:230
  44.1 11.5 %all-to-all-start.1 = ((f32[32,8,128]{2,1,0:T(8,128)}), f32[32,8,128]{2,1,0:T(8,128)S(1)}, u32[]{:S(2)}, u32[]{:S(2)}) async-start(f32[32,8,128]{2,1,0:T(8,128)} %bitcast.4), calls=%async_computation.1 | async-start | bytes 262144 | tf_op jit(solution)/shard_map/all_to_all | solution.py:252
  48.0 9.1 %collective-permute-start.1 = (f32[8,512]{1,0:T(8,128)S(1)}, f32[8,512]{1,0:T(8,128)S(1)}, u32[]{:S(2)}, u32[]{:S(2)}) collective-permute-start(f32[8,512]{1,0:T(8,128)S(1)} %get-tuple-element.17), channel_id=1, source_target_pairs={{0,1},{1,0},{2,3},{3,2},{4,5},{5,4},{6,7},{7,6},{8,9},{9,8},{10,11... | collective-permute-start | bytes 49160 | tf_op jit(solution)/shard_map/ppermute | solution.py:257
  55.7 2.3 %collective-permute-start.2 = (f32[8,128]{1,0:T(8,128)S(1)}, f32[8,128]{1,0:T(8,128)S(1)}, u32[]{:S(2)}, u32[]{:S(2)}) collective-permute-start(f32[8,128]{1,0:T(8,128)S(1)} %reduce_sum.18), channel_id=1, source_target_pairs={{0,2},{2,0},{1,3},{3,1},{4,6},{6,4},{5,7},{7,5},{8,10},{10,8},{9,1... | collective-permute-start | bytes 12296 | tf_op jit(solution)/shard_map/ppermute | solution.py:254
  72.5 8.6 %collective-permute-start.3 = (f32[32,40,128]{2,1,0:T(8,128)S(1)}, f32[32,40,128]{2,1,0:T(8,128)S(1)}, u32[]{:S(2)}, u32[]{:S(2)}) collective-permute-start(f32[32,40,128]{2,1,0:T(8,128)S(1)} %all_to_all.21.own_ref), channel_id=1, source_target_pairs={{0,2},{2,0},{1,3},{3,1},{4,6},{6,4},{5,7},{7,5},{8,10},{10,8},{9,1... | collective-permute-start | bytes 1966088 | tf_op jit(solution)/shard_map/ppermute | solution.py:230
  94.8 11.5 %all-to-all-start.3 = ((f32[32,8,128]{2,1,0:T(8,128)}), f32[32,8,128]{2,1,0:T(8,128)S(1)}, u32[]{:S(2)}, u32[]{:S(2)}) async-start(f32[32,8,128]{2,1,0:T(8,128)} %bitcast.5), calls=%async_computation.3 | async-start | bytes 262144 | tf_op jit(solution)/shard_map/all_to_all | solution.py:252
  98.7 9.1 %collective-permute-start.4 = (f32[8,512]{1,0:T(8,128)S(1)}, f32[8,512]{1,0:T(8,128)S(1)}, u32[]{:S(2)}, u32[]{:S(2)}) collective-permute-start(f32[8,512]{1,0:T(8,128)S(1)} %get-tuple-element.20), channel_id=1, source_target_pairs={{0,1},{1,0},{2,3},{3,2},{4,5},{5,4},{6,7},{7,6},{8,9},{9,8},{10,11... | collective-permute-start | bytes 49160 | tf_op jit(solution)/shard_map/ppermute | solution.py:257
  106.3 2.3 %collective-permute-start.5 = (f32[8,128]{1,0:T(8,128)S(1)}, f32[8,128]{1,0:T(8,128)S(1)}, u32[]{:S(2)}, u32[]{:S(2)}) collective-permute-start(f32[8,128]{1,0:T(8,128)S(1)} %reduce_sum.19), channel_id=1, source_target_pairs={{0,2},{2,0},{1,3},{3,1},{4,6},{6,4},{5,7},{7,5},{8,10},{10,8},{9,1... | collective-permute-start | bytes 12296 | tf_op jit(solution)/shard_map/ppermute | solution.py:254

commit v4 on v3

--- a/solution.py
+++ b/solution.py
@@ -67,12 +67,12 @@
     table_parts(own_ref, t2)
 
     def step(i, _):
-        for k, x in enumerate((xa, xb)):
-            s = i * 2 + k
+        for k, x in enumerate((xa, xb) * 8):
+            s = i * 16 + k
             e_ref[s] = look_up(t2, x, idx_ref[pl.ds(s, 1), :], par)
         return 0
 
-    lax.fori_loop(0, 8, step, 0)
+    lax.fori_loop(0, 1, step, 0)
 
 
 def main_kernel(
@@ -152,16 +152,34 @@
     look(0, xa, ya, ea, wa)
 
     def step(i, _):
-        s = 2 * i
+        s = 8 * i
         look(s + 1, xb, yb, eb, wb)
         scatter(jnp.maximum(s - 1, 0), vb)
         contract(s, ea, wa, va)
-        look(jnp.minimum(s + 2, 15), xa, ya, ea, wa)
+        look(s + 2, xa, ya, ea, wa)
         scatter(s, va)
         contract(s + 1, eb, wb, vb)
+        look(s + 3, xb, yb, eb, wb)
+        scatter(s + 1, vb)
+        contract(s + 2, ea, wa, va)
+        look(s + 4, xa, ya, ea, wa)
+        scatter(s + 2, va)
+        contract(s + 3, eb, wb, vb)
+        look(s + 5, xb, yb, eb, wb)
+        scatter(s + 3, vb)
+        contract(s + 4, ea, wa, va)
+        look(s + 6, xa, ya, ea, wa)
+        scatter(s + 4, va)
+        contract(s + 5, eb, wb, vb)
+        look(s + 7, xb, yb, eb, wb)
+        scatter(s + 5, vb)
+        contract(s + 6, ea, wa, va)
+        look(jnp.minimum(s + 8, 15), xa, ya, ea, wa)
+        scatter(s + 6, va)
+        contract(s + 7, eb, wb, vb)
         return 0
 
-    lax.fori_loop(0, 8, step, 0)
+    lax.fori_loop(0, 2, step, 0)
     scatter(15, vb)
     for m in range(8):
         c_ref[m : m + 1, :] = jnp.sum(cacc[m], axis=0, keepdims=True)

time: 110 us -> 106 us (0.964)
  Pallas kernels: 40.1 us -> 36.5 us
    pallas_call x2, Pallas kernels: 11.9 us -> 9.76 us  [phase(): pl.pallas_call(own_kernel, out_shape=pltpu.VMEM((16, 8, 512), F32), in_sp...]
    pallas_call x2, Pallas kernels: 27.4 us -> 25.9 us  [phase(): pl.pallas_call(functools.partial(main_kernel, merge), out_shape=(pltpu.VM...]
  transfers between devices with their start and end apart: 8 -> 8, of which waited for: 4 -> 4; matrix products, arithmetic and copies ran while one was open for 1% -> 1% of each run, Pallas kernels for 11% -> 9%
where the time goes in v4:
time: 106 us
  Pallas kernels  36.5 us (34%)
  blocking collectives  34.7 us (33%)
  starting transfers between devices  22.9 us (22%)
  waiting for transfers between devices  9.45 us (9%)
  other arithmetic  1.37 us (1%)
    all_to_all x2, blocking collectives, gather_all(): own = lax.all_to_all(send, CHIPS, 0, 0, tiled=True)  34.7 us
    pallas_call x2, Pallas kernels, phase(): pl.pallas_call(functools.partial(main_kernel, merge), out_shape=(pltpu.VM...  25.9 us
    pallas_call x2, Pallas kernels, phase(): pl.pallas_call(own_kernel, out_shape=pltpu.VMEM((16, 8, 512), F32), in_sp...  9.76 us
    all_to_all x2, waiting for transfers between devices, reduce_gen(): got = lax.all_to_all(gen, CHIPS, 0, 0, tiled=True)  8.42 us
    all_to_all x2, starting transfers between devices, reduce_gen(): got = lax.all_to_all(gen, CHIPS, 0, 0, tiled=True)  7.75 us
    ppermute x2, starting transfers between devices, add_br(): other = lax.ppermute(c, 'br', SWAP)  6.77 us
    ppermute x2, starting transfers between devices, gather_all(): return (own, lax.ppermute(own, 'c', SWAP))  5.39 us
    ppermute x2, starting transfers between devices, reduce_gen(): return (got + lax.ppermute(got, 'c', SWAP)) / 16.0  3.02 us
  transfers between devices with their start and end apart: 8, of which 4 were waited for; matrix products, arithmetic and copies ran while one was open for 1% of the time, Pallas kernels for 9%

profile of v4, /device:TPU:1, one launch (start us, length us, event | category | flops | bytes accessed | tf_op | source)
XLA Modules:
  0.0 105.8 jit_solution(2643080851726177805)
XLA Ops:
  0.6 0.9 start.1
  1.5 20.3 %all_to_all.20.own_ref = f32[32,40,128]{2,1,0:T(8,128)S(1)} all-to-all(f32[32,40,128]{2,1,0:T(8,128)S(1)} %get-tuple-element.13), channel_id=1, replica_groups=mesh['y'=4,'zl'=2,'x'=4,'c'=2,'br'=2] {'y','zl','x'}, dimensions={0} | all-to-all | bytes 1310720 | tf_op jit(solution)/shard_map/all_to_all | solution.py:247
  21.8 2.7 %collective-permute-start = (f32[32,40,128]{2,1,0:T(8,128)S(1)}, f32[32,40,128]{2,1,0:T(8,128)S(1)}, u32[]{:S(2)}, u32[]{:S(2)}) collective-permute-start(f32[32,40,128]{2,1,0:T(8,128)S(1)} %all_to_all.20.own_ref), channel_id=1, source_target_pairs={{0,2},{2,0},{1,3},{3,1},{4,6},{6,4},{5,7},{7,5},{8,10},{10,8},{9,1... | collective-permute-start | bytes 1966088 | tf_op jit(solution)/shard_map/ppermute | solution.py:248
  24.5 4.9 %own.2.e_ref = f32[16,8,512]{2,1,0:T(8,128)S(1)} custom-call(s32[1]{0:T(128)} %bitcast.par_ref, f32[32,40,128]{2,1,0:T(8,128)S(1)} %all_to_all.20.own_ref, s32[16,512]{1,0:T(8,128)S(1)} %get-tuple-element.14.idx_ref), custom_call_target="tpu_custom_call" | custom-call | tf_op jit(solution)/shard_map/own/pallas_call | solution.py:211
  29.4 0.0 collective-permute-done.oth_ref
  29.4 12.9 %main.2 = (f32[8,512]{1,0:T(8,128)S(1)}, f32[16,2,8,128]{3,2,1,0:T(8,128)}, f32[8,128]{1,0:T(8,128)S(1)}) custom-call(s32[1]{0:T(128)} %bitcast.par_ref, f32[32,40,128]{2,1,0:T(8,128)S(1)} %all_to_all.20.own_ref, f32[32,40,128]{2,1,0:T(8,128)S(1)} %collective-permute-done.oth_ref, f32[16,8,512]{2,1,0:T(8,128)S(1)} %own.2.e_ref, ...), custom_call_target="tpu_custom_call" | custom-call | tf_op jit(solution)/shard_map/main/pallas_call | solution.py:220
  42.3 3.9 %all-to-all-start.1 = ((f32[32,8,128]{2,1,0:T(8,128)}), f32[32,8,128]{2,1,0:T(8,128)S(1)}, u32[]{:S(2)}, u32[]{:S(2)}) async-start(f32[32,8,128]{2,1,0:T(8,128)} %bitcast.4), calls=%async_computation.1 | async-start | bytes 262144 | tf_op jit(solution)/shard_map/all_to_all | solution.py:270
  46.2 3.4 %collective-permute-start.1 = (f32[8,512]{1,0:T(8,128)S(1)}, f32[8,512]{1,0:T(8,128)S(1)}, u32[]{:S(2)}, u32[]{:S(2)}) collective-permute-start(f32[8,512]{1,0:T(8,128)S(1)} %get-tuple-element.17), channel_id=1, source_target_pairs={{0,1},{1,0},{2,3},{3,2},{4,5},{5,4},{6,7},{7,6},{8,9},{9,8},{10,11... | collective-permute-start | bytes 49160 | tf_op jit(solution)/shard_map/ppermute | solution.py:275
  49.6 4.2 %all-to-all-done.1 = f32[32,8,128]{2,1,0:T(8,128)S(1)} async-done(((f32[32,8,128]{2,1,0:T(8,128)}), f32[32,8,128]{2,1,0:T(8,128)S(1)}, u32[]{:S(2)}, u32[]{:S(2)}) %all-to-all-start.1) | async-done | bytes 131104 | tf_op jit(solution)/shard_map/all_to_all | solution.py:270
  53.9 1.5 %collective-permute-start.2 = (f32[8,128]{1,0:T(8,128)S(1)}, f32[8,128]{1,0:T(8,128)S(1)}, u32[]{:S(2)}, u32[]{:S(2)}) collective-permute-start(f32[8,128]{1,0:T(8,128)S(1)} %reduce_sum.18), channel_id=1, source_target_pairs={{0,2},{2,0},{1,3},{3,1},{4,6},{6,4},{5,7},{7,5},{8,10},{10,8},{9,1... | collective-permute-start | bytes 12296 | tf_op jit(solution)/shard_map/ppermute | solution.py:272
  55.4 0.0 collective-permute-done.1
  55.4 0.8 collective-permute-done.2
  56.3 14.4 %all_to_all.21.own_ref = f32[32,40,128]{2,1,0:T(8,128)S(1)} all-to-all(f32[32,40,128]{2,1,0:T(8,128)S(1)} %broadcast_in_dim.2), channel_id=1, replica_groups=mesh['y'=4,'zl'=2,'x'=4,'c'=2,'br'=2] {'y','zl','x'}, dimensions={0} | all-to-all | bytes 1310720 | tf_op jit(solution)/shard_map/all_to_all | solution.py:247
  70.7 2.7 %collective-permute-start.3 = (f32[32,40,128]{2,1,0:T(8,128)S(1)}, f32[32,40,128]{2,1,0:T(8,128)S(1)}, u32[]{:S(2)}, u32[]{:S(2)}) collective-permute-start(f32[32,40,128]{2,1,0:T(8,128)S(1)} %all_to_all.21.own_ref), channel_id=1, source_target_pairs={{0,2},{2,0},{1,3},{3,1},{4,6},{6,4},{5,7},{7,5},{8,10},{10,8},{9,1... | collective-permute-start | bytes 1966088 | tf_op jit(solution)/shard_map/ppermute | solution.py:248
  73.4 4.9 %own.3.e_ref = f32[16,8,512]{2,1,0:T(8,128)S(1)} custom-call(s32[1]{0:T(128)} %bitcast.par_ref, f32[32,40,128]{2,1,0:T(8,128)S(1)} %all_to_all.21.own_ref, s32[16,512]{1,0:T(8,128)S(1)} %get-tuple-element.14.idx_ref), custom_call_target="tpu_custom_call" | custom-call | tf_op jit(solution)/shard_map/own/pallas_call | solution.py:211
  78.3 0.0 collective-permute-done.3.oth_ref
  78.3 13.0 %main.3 = (f32[8,512]{1,0:T(8,128)S(1)}, f32[16,2,8,128]{3,2,1,0:T(8,128)}, f32[8,128]{1,0:T(8,128)}) custom-call(s32[1]{0:T(128)} %bitcast.par_ref, f32[32,40,128]{2,1,0:T(8,128)S(1)} %all_to_all.21.own_ref, f32[32,40,128]{2,1,0:T(8,128)S(1)} %collective-permute-done.3.oth_ref, f32[16,8,512]{2,1,0:T(8,128)S(1)} %own.3.e_ref, ...), custom_call_target="tpu_custom_call" | custom-call | tf_op jit(solution)/shard_map/main/pallas_call | solution.py:220
  91.3 3.9 %all-to-all-start.3 = ((f32[32,8,128]{2,1,0:T(8,128)}), f32[32,8,128]{2,1,0:T(8,128)S(1)}, u32[]{:S(2)}, u32[]{:S(2)}) async-start(f32[32,8,128]{2,1,0:T(8,128)} %bitcast.5), calls=%async_computation.3 | async-start | bytes 262144 | tf_op jit(solution)/shard_map/all_to_all | solution.py:270
  95.1 3.4 %collective-permute-start.4 = (f32[8,512]{1,0:T(8,128)S(1)}, f32[8,512]{1,0:T(8,128)S(1)}, u32[]{:S(2)}, u32[]{:S(2)}) collective-permute-start(f32[8,512]{1,0:T(8,128)S(1)} %get-tuple-element.20), channel_id=1, source_target_pairs={{0,1},{1,0},{2,3},{3,2},{4,5},{5,4},{6,7},{7,6},{8,9},{9,8},{10,11... | collective-permute-start | bytes 49160 | tf_op jit(solution)/shard_map/ppermute | solution.py:275
  98.5 4.2 %all-to-all-done.3 = f32[32,8,128]{2,1,0:T(8,128)S(1)} async-done(((f32[32,8,128]{2,1,0:T(8,128)}), f32[32,8,128]{2,1,0:T(8,128)S(1)}, u32[]{:S(2)}, u32[]{:S(2)}) %all-to-all-start.3) | async-done | bytes 131104 | tf_op jit(solution)/shard_map/all_to_all | solution.py:270
  102.8 1.5 %collective-permute-start.5 = (f32[8,128]{1,0:T(8,128)S(1)}, f32[8,128]{1,0:T(8,128)S(1)}, u32[]{:S(2)}, u32[]{:S(2)}) collective-permute-start(f32[8,128]{1,0:T(8,128)S(1)} %reduce_sum.19), channel_id=1, source_target_pairs={{0,2},{2,0},{1,3},{3,1},{4,6},{6,4},{5,7},{7,5},{8,10},{10,8},{9,1... | collective-permute-start | bytes 12296 | tf_op jit(solution)/shard_map/ppermute | solution.py:272
  104.3 0.0 collective-permute-done.4
  104.3 0.6 add.34
  104.9 0.2 collective-permute-done.5
  105.1 0.7 slice_select_fusion
  (7 shorter events, 0.1 us)
Async XLA Ops:
  21.8 7.6 %collective-permute-start = (f32[32,40,128]{2,1,0:T(8,128)S(1)}, f32[32,40,128]{2,1,0:T(8,128)S(1)}, u32[]{:S(2)}, u32[]{:S(2)}) collective-permute-start(f32[32,40,128]{2,1,0:T(8,128)S(1)} %all_to_all.20.own_ref), channel_id=1, source_target_pairs={{0,2},{2,0},{1,3},{3,1},{4,6},{6,4},{5,7},{7,5},{8,10},{10,8},{9,1... | collective-permute-start | bytes 1966088 | tf_op jit(solution)/shard_map/ppermute | solution.py:248
  42.3 11.5 %all-to-all-start.1 = ((f32[32,8,128]{2,1,0:T(8,128)}), f32[32,8,128]{2,1,0:T(8,128)S(1)}, u32[]{:S(2)}, u32[]{:S(2)}) async-start(f32[32,8,128]{2,1,0:T(8,128)} %bitcast.4), calls=%async_computation.1 | async-start | bytes 262144 | tf_op jit(solution)/shard_map/all_to_all | solution.py:270
  46.2 9.1 %collective-permute-start.1 = (f32[8,512]{1,0:T(8,128)S(1)}, f32[8,512]{1,0:T(8,128)S(1)}, u32[]{:S(2)}, u32[]{:S(2)}) collective-permute-start(f32[8,512]{1,0:T(8,128)S(1)} %get-tuple-element.17), channel_id=1, source_target_pairs={{0,1},{1,0},{2,3},{3,2},{4,5},{5,4},{6,7},{7,6},{8,9},{9,8},{10,11... | collective-permute-start | bytes 49160 | tf_op jit(solution)/shard_map/ppermute | solution.py:275
  53.9 2.3 %collective-permute-start.2 = (f32[8,128]{1,0:T(8,128)S(1)}, f32[8,128]{1,0:T(8,128)S(1)}, u32[]{:S(2)}, u32[]{:S(2)}) collective-permute-start(f32[8,128]{1,0:T(8,128)S(1)} %reduce_sum.18), channel_id=1, source_target_pairs={{0,2},{2,0},{1,3},{3,1},{4,6},{6,4},{5,7},{7,5},{8,10},{10,8},{9,1... | collective-permute-start | bytes 12296 | tf_op jit(solution)/shard_map/ppermute | solution.py:272
  70.7 7.6 %collective-permute-start.3 = (f32[32,40,128]{2,1,0:T(8,128)S(1)}, f32[32,40,128]{2,1,0:T(8,128)S(1)}, u32[]{:S(2)}, u32[]{:S(2)}) collective-permute-start(f32[32,40,128]{2,1,0:T(8,128)S(1)} %all_to_all.21.own_ref), channel_id=1, source_target_pairs={{0,2},{2,0},{1,3},{3,1},{4,6},{6,4},{5,7},{7,5},{8,10},{10,8},{9,1... | collective-permute-start | bytes 1966088 | tf_op jit(solution)/shard_map/ppermute | solution.py:248
  91.3 11.5 %all-to-all-start.3 = ((f32[32,8,128]{2,1,0:T(8,128)}), f32[32,8,128]{2,1,0:T(8,128)S(1)}, u32[]{:S(2)}, u32[]{:S(2)}) async-start(f32[32,8,128]{2,1,0:T(8,128)} %bitcast.5), calls=%async_computation.3 | async-start | bytes 262144 | tf_op jit(solution)/shard_map/all_to_all | solution.py:270
  95.1 9.1 %collective-permute-start.4 = (f32[8,512]{1,0:T(8,128)S(1)}, f32[8,512]{1,0:T(8,128)S(1)}, u32[]{:S(2)}, u32[]{:S(2)}) collective-permute-start(f32[8,512]{1,0:T(8,128)S(1)} %get-tuple-element.20), channel_id=1, source_target_pairs={{0,1},{1,0},{2,3},{3,2},{4,5},{5,4},{6,7},{7,6},{8,9},{9,8},{10,11... | collective-permute-start | bytes 49160 | tf_op jit(solution)/shard_map/ppermute | solution.py:275
  102.8 2.3 %collective-permute-start.5 = (f32[8,128]{1,0:T(8,128)S(1)}, f32[8,128]{1,0:T(8,128)S(1)}, u32[]{:S(2)}, u32[]{:S(2)}) collective-permute-start(f32[8,128]{1,0:T(8,128)S(1)} %reduce_sum.19), channel_id=1, source_target_pairs={{0,2},{2,0},{1,3},{3,1},{4,6},{6,4},{5,7},{7,5},{8,10},{10,8},{9,1... | collective-permute-start | bytes 12296 | tf_op jit(solution)/shard_map/ppermute | solution.py:272

commit v5 on v4

--- a/solution.py
+++ b/solution.py
@@ -22,6 +22,16 @@
 def rows_are(sel, index):
     io = lax.broadcasted_iota(I32, (sel, index.shape[1]), 0)
     return jnp.where(io == index, 1.0, 0.0).astype(BF16)
+
+
+def rows_like(io, sel, index):
+    blocks = []
+    for base in range(0, sel, 256):
+        rel = jnp.broadcast_to((index - base).astype(F32), (16, index.shape[1])).astype(BF16)
+        for b in range(16):
+            row = jnp.concatenate([io[b * 16 : b * 16 + 16, :]] * (index.shape[1] // 128), axis=1)
+            blocks.append(jnp.where(row == rel, jnp.ones_like(rel), jnp.zeros_like(rel)))
+    return jnp.concatenate(blocks, axis=0)
 
 
 def table_parts(tab_ref, t2):
@@ -41,9 +51,10 @@
     return hi + lo
 
 
-def look_up(t2, x, row, parity):
+def look_up(t2, x, row, parity, io=None):
     lo = jnp.where(((row >> 9) & 1) == parity, row & 511, -1)
-    x[...] = jnp.dot(t2.reshape(512, 512)[...], rows_are(512, lo), preferred_element_type=F32)
+    oh = rows_are(512, lo) if io is None else rows_like(io, 512, lo)
+    x[...] = jnp.dot(t2.reshape(512, 512)[...], oh, preferred_element_type=F32)
     return pick(32, row >> 10, x)
 
 
@@ -77,7 +88,7 @@
 
 def main_kernel(
     merge, par_ref, own_ref, oth_ref, e_ref, f_ref, win_ref, idx_ref, q_ref, g_hbm,
-    c_ref, gen_ref, pc_ref, g_ref, t2, p2, xa, ya, xb, yb, ea, wa, va, eb, wb, vb, fw, cacc, gacc, sems,
+    c_ref, gen_ref, pc_ref, g_ref, t2, p2, xa, ya, xb, yb, ea, wa, va, eb, wb, vb, fw, cacc, gacc, io, sems,
 ):
     for s in range(16):
         pltpu.make_async_copy(g_hbm.at[s], g_ref.at[s], sems.at[s]).start()
@@ -100,6 +111,7 @@
         fw[0, m] = wm * (1.0 - fm)
         fw[1, m] = wm
         fw[2, m] = fm
+    io[...] = lax.broadcasted_iota(I32, (256, 128), 0).astype(F32).astype(BF16)
     cacc[...] = jnp.zeros_like(cacc)
     gacc[...] = jnp.zeros_like(gacc)
     va[...] = jnp.zeros_like(va)
@@ -108,9 +120,9 @@
     def look(s, x, y, e_s, w_s):
         qrow = q_ref[pl.ds(s, 1), :]
         y[...] = jnp.dot(
-            p2.reshape(256, 256)[...], rows_are(256, qrow & 255), preferred_element_type=F32
+            p2.reshape(256, 256)[...], rows_like(io, 256, qrow & 255), preferred_element_type=F32
         )
-        e_s[...] = look_up(t2, x, idx_ref[pl.ds(s, 1), :], other) + e_ref[s]
+        e_s[...] = look_up(t2, x, idx_ref[pl.ds(s, 1), :], other, io) + e_ref[s]
         w_s[...] = pick(16, qrow >> 8, y)
 
     def contract(s, e_s, w_s, v_s):
@@ -139,13 +151,11 @@
         v = v_s[...]
         v1 = v.astype(BF16).astype(F32)
         v2 = v - v1
-        hm = lax.broadcasted_iota(I32, (16, 8, 512), 0) == (qrow >> 8)[None]
-        a = [
-            jnp.where(hm, jnp.broadcast_to(vv[None], (16, 8, 512)), 0.0).astype(BF16).reshape(128, 512)
-            for vv in (v1, v2)
-        ]
+        v12 = jnp.concatenate([v1, v2], axis=0).astype(BF16)
+        hq = jnp.broadcast_to((qrow >> 8).astype(F32), (16, 512)).astype(BF16)
+        a = [jnp.where(hq == jnp.full_like(hq, r), v12, jnp.zeros_like(v12)) for r in range(16)]
         gacc[...] += lax.dot_general(
-            jnp.concatenate(a, axis=0), rows_are(256, qrow & 255), (((1,), (1,)), ((), ())),
+            jnp.concatenate(a, axis=0), rows_like(io, 256, qrow & 255), (((1,), (1,)), ((), ())),
             preferred_element_type=F32,
         )
 
@@ -183,7 +193,8 @@
     scatter(15, vb)
     for m in range(8):
         c_ref[m : m + 1, :] = jnp.sum(cacc[m], axis=0, keepdims=True)
-    gs = (gacc[0:128] + gacc[128:256]).reshape(16, 8, 256)
+    gs = gacc[...].reshape(16, 2, 8, 256)
+    gs = gs[:, 0] + gs[:, 1]
     for h in range(2):
         gen_ref[:, h] = gs[:, :, h * 128 : (h + 1) * 128]
 
@@ -231,6 +242,7 @@
             pltpu.VMEM((3, 8, 8, 512), F32),
             pltpu.VMEM((8, 8, 512), F32),
             pltpu.VMEM((256, 256), F32),
+            pltpu.VMEM((256, 128), BF16),
             pltpu.SemaphoreType.DMA((16,)),
         ],
         compiler_params=pltpu.CompilerParams(vmem_limit_bytes=24 << 20),

time: 106 us -> 105 us (level)
  no operation moved by 1% of the time
where the time goes in v5:
time: 105 us
  Pallas kernels  35.7 us (34%)
  blocking collectives  34.7 us (33%)
  starting transfers between devices  22.9 us (22%)
  waiting for transfers between devices  9.45 us (9%)
  other arithmetic  1.37 us (1%)
    all_to_all x2, blocking collectives, gather_all(): own = lax.all_to_all(send, CHIPS, 0, 0, tiled=True)  34.7 us
    pallas_call x2, Pallas kernels, phase(): pl.pallas_call(functools.partial(main_kernel, merge), out_shape=(pltpu.VM...  25.1 us
    pallas_call x2, Pallas kernels, phase(): pl.pallas_call(own_kernel, out_shape=pltpu.VMEM((16, 8, 512), F32), in_sp...  9.76 us
    all_to_all x2, waiting for transfers between devices, reduce_gen(): got = lax.all_to_all(gen, CHIPS, 0, 0, tiled=True)  8.42 us
    all_to_all x2, starting transfers between devices, reduce_gen(): got = lax.all_to_all(gen, CHIPS, 0, 0, tiled=True)  7.74 us
    ppermute x2, starting transfers between devices, add_br(): other = lax.ppermute(c, 'br', SWAP)  6.76 us
    ppermute x2, starting transfers between devices, gather_all(): return (own, lax.ppermute(own, 'c', SWAP))  5.38 us
    ppermute x2, starting transfers between devices, reduce_gen(): return (got + lax.ppermute(got, 'c', SWAP)) / 16.0  3.05 us
  transfers between devices with their start and end apart: 8, of which 4 were waited for; matrix products, arithmetic and copies ran while one was open for 1% of the time, Pallas kernels for 9%

profile of v5, /device:TPU:1, one launch (start us, length us, event | category | flops | bytes accessed | tf_op | source)
XLA Modules:
  0.0 104.9 jit_solution(18117791230739233422)
XLA Ops:
  0.6 0.9 start.1
  1.5 20.3 %all_to_all.20.own_ref = f32[32,40,128]{2,1,0:T(8,128)S(1)} all-to-all(f32[32,40,128]{2,1,0:T(8,128)S(1)} %get-tuple-element.13), channel_id=1, replica_groups=mesh['y'=4,'zl'=2,'x'=4,'c'=2,'br'=2] {'y','zl','x'}, dimensions={0} | all-to-all | bytes 1310720 | tf_op jit(solution)/shard_map/all_to_all | solution.py:259
  21.8 2.7 %collective-permute-start = (f32[32,40,128]{2,1,0:T(8,128)S(1)}, f32[32,40,128]{2,1,0:T(8,128)S(1)}, u32[]{:S(2)}, u32[]{:S(2)}) collective-permute-start(f32[32,40,128]{2,1,0:T(8,128)S(1)} %all_to_all.20.own_ref), channel_id=1, source_target_pairs={{0,2},{2,0},{1,3},{3,1},{4,6},{6,4},{5,7},{7,5},{8,10},{10,8},{9,1... | collective-permute-start | bytes 1966088 | tf_op jit(solution)/shard_map/ppermute | solution.py:260
  24.5 4.9 %own.2.e_ref = f32[16,8,512]{2,1,0:T(8,128)S(1)} custom-call(s32[1]{0:T(128)} %bitcast.par_ref, f32[32,40,128]{2,1,0:T(8,128)S(1)} %all_to_all.20.own_ref, s32[16,512]{1,0:T(8,128)S(1)} %get-tuple-element.14.idx_ref), custom_call_target="tpu_custom_call" | custom-call | tf_op jit(solution)/shard_map/own/pallas_call | solution.py:222
  29.4 0.0 collective-permute-done.oth_ref
  29.4 12.5 %main.2 = (f32[8,512]{1,0:T(8,128)S(1)}, f32[16,2,8,128]{3,2,1,0:T(8,128)}, f32[8,128]{1,0:T(8,128)S(1)}) custom-call(s32[1]{0:T(128)} %bitcast.par_ref, f32[32,40,128]{2,1,0:T(8,128)S(1)} %all_to_all.20.own_ref, f32[32,40,128]{2,1,0:T(8,128)S(1)} %collective-permute-done.oth_ref, f32[16,8,512]{2,1,0:T(8,128)S(1)} %own.2.e_ref, ...), custom_call_target="tpu_custom_call" | custom-call | tf_op jit(solution)/shard_map/main/pallas_call | solution.py:231
  41.9 3.9 %all-to-all-start.1 = ((f32[32,8,128]{2,1,0:T(8,128)}), f32[32,8,128]{2,1,0:T(8,128)S(1)}, u32[]{:S(2)}, u32[]{:S(2)}) async-start(f32[32,8,128]{2,1,0:T(8,128)} %bitcast.4), calls=%async_computation.1 | async-start | bytes 262144 | tf_op jit(solution)/shard_map/all_to_all | solution.py:282
  45.8 3.4 %collective-permute-start.1 = (f32[8,512]{1,0:T(8,128)S(1)}, f32[8,512]{1,0:T(8,128)S(1)}, u32[]{:S(2)}, u32[]{:S(2)}) collective-permute-start(f32[8,512]{1,0:T(8,128)S(1)} %get-tuple-element.17), channel_id=1, source_target_pairs={{0,1},{1,0},{2,3},{3,2},{4,5},{5,4},{6,7},{7,6},{8,9},{9,8},{10,11... | collective-permute-start | bytes 49160 | tf_op jit(solution)/shard_map/ppermute | solution.py:287
  49.2 4.2 %all-to-all-done.1 = f32[32,8,128]{2,1,0:T(8,128)S(1)} async-done(((f32[32,8,128]{2,1,0:T(8,128)}), f32[32,8,128]{2,1,0:T(8,128)S(1)}, u32[]{:S(2)}, u32[]{:S(2)}) %all-to-all-start.1) | async-done | bytes 131104 | tf_op jit(solution)/shard_map/all_to_all | solution.py:282
  53.4 1.5 %collective-permute-start.2 = (f32[8,128]{1,0:T(8,128)S(1)}, f32[8,128]{1,0:T(8,128)S(1)}, u32[]{:S(2)}, u32[]{:S(2)}) collective-permute-start(f32[8,128]{1,0:T(8,128)S(1)} %reduce_sum.18), channel_id=1, source_target_pairs={{0,2},{2,0},{1,3},{3,1},{4,6},{6,4},{5,7},{7,5},{8,10},{10,8},{9,1... | collective-permute-start | bytes 12296 | tf_op jit(solution)/shard_map/ppermute | solution.py:284
  54.9 0.0 collective-permute-done.1
  55.0 0.8 collective-permute-done.2
  55.8 14.5 %all_to_all.21.own_ref = f32[32,40,128]{2,1,0:T(8,128)S(1)} all-to-all(f32[32,40,128]{2,1,0:T(8,128)S(1)} %broadcast_in_dim.2), channel_id=1, replica_groups=mesh['y'=4,'zl'=2,'x'=4,'c'=2,'br'=2] {'y','zl','x'}, dimensions={0} | all-to-all | bytes 1310720 | tf_op jit(solution)/shard_map/all_to_all | solution.py:259
  70.3 2.7 %collective-permute-start.3 = (f32[32,40,128]{2,1,0:T(8,128)S(1)}, f32[32,40,128]{2,1,0:T(8,128)S(1)}, u32[]{:S(2)}, u32[]{:S(2)}) collective-permute-start(f32[32,40,128]{2,1,0:T(8,128)S(1)} %all_to_all.21.own_ref), channel_id=1, source_target_pairs={{0,2},{2,0},{1,3},{3,1},{4,6},{6,4},{5,7},{7,5},{8,10},{10,8},{9,1... | collective-permute-start | bytes 1966088 | tf_op jit(solution)/shard_map/ppermute | solution.py:260
  73.0 4.9 %own.3.e_ref = f32[16,8,512]{2,1,0:T(8,128)S(1)} custom-call(s32[1]{0:T(128)} %bitcast.par_ref, f32[32,40,128]{2,1,0:T(8,128)S(1)} %all_to_all.21.own_ref, s32[16,512]{1,0:T(8,128)S(1)} %get-tuple-element.14.idx_ref), custom_call_target="tpu_custom_call" | custom-call | tf_op jit(solution)/shard_map/own/pallas_call | solution.py:222
  77.9 0.0 collective-permute-done.3.oth_ref
  77.9 12.5 %main.3 = (f32[8,512]{1,0:T(8,128)S(1)}, f32[16,2,8,128]{3,2,1,0:T(8,128)}, f32[8,128]{1,0:T(8,128)}) custom-call(s32[1]{0:T(128)} %bitcast.par_ref, f32[32,40,128]{2,1,0:T(8,128)S(1)} %all_to_all.21.own_ref, f32[32,40,128]{2,1,0:T(8,128)S(1)} %collective-permute-done.3.oth_ref, f32[16,8,512]{2,1,0:T(8,128)S(1)} %own.3.e_ref, ...), custom_call_target="tpu_custom_call" | custom-call | tf_op jit(solution)/shard_map/main/pallas_call | solution.py:231
  90.4 3.9 %all-to-all-start.3 = ((f32[32,8,128]{2,1,0:T(8,128)}), f32[32,8,128]{2,1,0:T(8,128)S(1)}, u32[]{:S(2)}, u32[]{:S(2)}) async-start(f32[32,8,128]{2,1,0:T(8,128)} %bitcast.5), calls=%async_computation.3 | async-start | bytes 262144 | tf_op jit(solution)/shard_map/all_to_all | solution.py:282
  94.3 3.4 %collective-permute-start.4 = (f32[8,512]{1,0:T(8,128)S(1)}, f32[8,512]{1,0:T(8,128)S(1)}, u32[]{:S(2)}, u32[]{:S(2)}) collective-permute-start(f32[8,512]{1,0:T(8,128)S(1)} %get-tuple-element.20), channel_id=1, source_target_pairs={{0,1},{1,0},{2,3},{3,2},{4,5},{5,4},{6,7},{7,6},{8,9},{9,8},{10,11... | collective-permute-start | bytes 49160 | tf_op jit(solution)/shard_map/ppermute | solution.py:287
  97.7 4.2 %all-to-all-done.3 = f32[32,8,128]{2,1,0:T(8,128)S(1)} async-done(((f32[32,8,128]{2,1,0:T(8,128)}), f32[32,8,128]{2,1,0:T(8,128)S(1)}, u32[]{:S(2)}, u32[]{:S(2)}) %all-to-all-start.3) | async-done | bytes 131104 | tf_op jit(solution)/shard_map/all_to_all | solution.py:282
  101.9 1.5 %collective-permute-start.5 = (f32[8,128]{1,0:T(8,128)S(1)}, f32[8,128]{1,0:T(8,128)S(1)}, u32[]{:S(2)}, u32[]{:S(2)}) collective-permute-start(f32[8,128]{1,0:T(8,128)S(1)} %reduce_sum.19), channel_id=1, source_target_pairs={{0,2},{2,0},{1,3},{3,1},{4,6},{6,4},{5,7},{7,5},{8,10},{10,8},{9,1... | collective-permute-start | bytes 12296 | tf_op jit(solution)/shard_map/ppermute | solution.py:284
  103.4 0.0 collective-permute-done.4
  103.4 0.6 add.34
  104.1 0.2 collective-permute-done.5
  104.3 0.7 slice_select_fusion
  (7 shorter events, 0.1 us)
Async XLA Ops:
  21.8 7.6 %collective-permute-start = (f32[32,40,128]{2,1,0:T(8,128)S(1)}, f32[32,40,128]{2,1,0:T(8,128)S(1)}, u32[]{:S(2)}, u32[]{:S(2)}) collective-permute-start(f32[32,40,128]{2,1,0:T(8,128)S(1)} %all_to_all.20.own_ref), channel_id=1, source_target_pairs={{0,2},{2,0},{1,3},{3,1},{4,6},{6,4},{5,7},{7,5},{8,10},{10,8},{9,1... | collective-permute-start | bytes 1966088 | tf_op jit(solution)/shard_map/ppermute | solution.py:260
  41.9 11.5 %all-to-all-start.1 = ((f32[32,8,128]{2,1,0:T(8,128)}), f32[32,8,128]{2,1,0:T(8,128)S(1)}, u32[]{:S(2)}, u32[]{:S(2)}) async-start(f32[32,8,128]{2,1,0:T(8,128)} %bitcast.4), calls=%async_computation.1 | async-start | bytes 262144 | tf_op jit(solution)/shard_map/all_to_all | solution.py:282
  45.8 9.1 %collective-permute-start.1 = (f32[8,512]{1,0:T(8,128)S(1)}, f32[8,512]{1,0:T(8,128)S(1)}, u32[]{:S(2)}, u32[]{:S(2)}) collective-permute-start(f32[8,512]{1,0:T(8,128)S(1)} %get-tuple-element.17), channel_id=1, source_target_pairs={{0,1},{1,0},{2,3},{3,2},{4,5},{5,4},{6,7},{7,6},{8,9},{9,8},{10,11... | collective-permute-start | bytes 49160 | tf_op jit(solution)/shard_map/ppermute | solution.py:287
  53.4 2.3 %collective-permute-start.2 = (f32[8,128]{1,0:T(8,128)S(1)}, f32[8,128]{1,0:T(8,128)S(1)}, u32[]{:S(2)}, u32[]{:S(2)}) collective-permute-start(f32[8,128]{1,0:T(8,128)S(1)} %reduce_sum.18), channel_id=1, source_target_pairs={{0,2},{2,0},{1,3},{3,1},{4,6},{6,4},{5,7},{7,5},{8,10},{10,8},{9,1... | collective-permute-start | bytes 12296 | tf_op jit(solution)/shard_map/ppermute | solution.py:284
  70.3 7.6 %collective-permute-start.3 = (f32[32,40,128]{2,1,0:T(8,128)S(1)}, f32[32,40,128]{2,1,0:T(8,128)S(1)}, u32[]{:S(2)}, u32[]{:S(2)}) collective-permute-start(f32[32,40,128]{2,1,0:T(8,128)S(1)} %all_to_all.21.own_ref), channel_id=1, source_target_pairs={{0,2},{2,0},{1,3},{3,1},{4,6},{6,4},{5,7},{7,5},{8,10},{10,8},{9,1... | collective-permute-start | bytes 1966088 | tf_op jit(solution)/shard_map/ppermute | solution.py:260
  90.4 11.5 %all-to-all-start.3 = ((f32[32,8,128]{2,1,0:T(8,128)}), f32[32,8,128]{2,1,0:T(8,128)S(1)}, u32[]{:S(2)}, u32[]{:S(2)}) async-start(f32[32,8,128]{2,1,0:T(8,128)} %bitcast.5), calls=%async_computation.3 | async-start | bytes 262144 | tf_op jit(solution)/shard_map/all_to_all | solution.py:282
  94.3 9.2 %collective-permute-start.4 = (f32[8,512]{1,0:T(8,128)S(1)}, f32[8,512]{1,0:T(8,128)S(1)}, u32[]{:S(2)}, u32[]{:S(2)}) collective-permute-start(f32[8,512]{1,0:T(8,128)S(1)} %get-tuple-element.20), channel_id=1, source_target_pairs={{0,1},{1,0},{2,3},{3,2},{4,5},{5,4},{6,7},{7,6},{8,9},{9,8},{10,11... | collective-permute-start | bytes 49160 | tf_op jit(solution)/shard_map/ppermute | solution.py:287
  101.9 2.4 %collective-permute-start.5 = (f32[8,128]{1,0:T(8,128)S(1)}, f32[8,128]{1,0:T(8,128)S(1)}, u32[]{:S(2)}, u32[]{:S(2)}) collective-permute-start(f32[8,128]{1,0:T(8,128)S(1)} %reduce_sum.19), channel_id=1, source_target_pairs={{0,2},{2,0},{1,3},{3,1},{4,6},{6,4},{5,7},{7,5},{8,10},{10,8},{9,1... | collective-permute-start | bytes 12296 | tf_op jit(solution)/shard_map/ppermute | solution.py:284

commit v6 on v5

--- a/solution.py
+++ b/solution.py
@@ -73,14 +73,15 @@
     win_out[...] = win_ref[...]
 
 
-def own_kernel(par_ref, own_ref, idx_ref, e_ref, t2, xa, xb):
+def own_kernel(par_ref, own_ref, idx_ref, e_ref, t2, xa, xb, io):
+    io[...] = lax.broadcasted_iota(I32, (256, 128), 0).astype(F32).astype(BF16)
     par = par_ref[0] & 1
     table_parts(own_ref, t2)
 
     def step(i, _):
         for k, x in enumerate((xa, xb) * 8):
             s = i * 16 + k
-            e_ref[s] = look_up(t2, x, idx_ref[pl.ds(s, 1), :], par)
+            e_ref[s] = look_up(t2, x, idx_ref[pl.ds(s, 1), :], par, io)
         return 0
 
     lax.fori_loop(0, 1, step, 0)
@@ -216,6 +217,7 @@
         pltpu.VMEM((32, 2, 8, 512), BF16),
         pltpu.VMEM((512, 512), F32),
         pltpu.VMEM((512, 512), F32),
+        pltpu.VMEM((256, 128), BF16),
     ]
     own, oth, f, win, idx, q = map(in_vmem, (own, oth, f, win, idx, q))
     g = in_hbm(g)

time: 105 us -> 105 us (level)
  no operation moved by 1% of the time
where the time goes in v6:
time: 105 us; the launch traced here: 104 us
  Pallas kernels  35 us (33%)
  blocking collectives  34.7 us (33%)
  starting transfers between devices  22.9 us (22%)
  waiting for transfers between devices  9.44 us (9%)
  other arithmetic  1.37 us (1%)
    all_to_all x2, blocking collectives, gather_all(): own = lax.all_to_all(send, CHIPS, 0, 0, tiled=True)  34.7 us
    pallas_call x2, Pallas kernels, phase(): pl.pallas_call(functools.partial(main_kernel, merge), out_shape=(pltpu.VM...  25 us
    pallas_call x2, Pallas kernels, phase(): pl.pallas_call(own_kernel, out_shape=pltpu.VMEM((16, 8, 512), F32), in_sp...  9.11 us
    all_to_all x2, waiting for transfers between devices, reduce_gen(): got = lax.all_to_all(gen, CHIPS, 0, 0, tiled=True)  8.4 us
    all_to_all x2, starting transfers between devices, reduce_gen(): got = lax.all_to_all(gen, CHIPS, 0, 0, tiled=True)  7.75 us
    ppermute x2, starting transfers between devices, add_br(): other = lax.ppermute(c, 'br', SWAP)  6.78 us
    ppermute x2, starting transfers between devices, gather_all(): return (own, lax.ppermute(own, 'c', SWAP))  5.38 us
    ppermute x2, starting transfers between devices, reduce_gen(): return (got + lax.ppermute(got, 'c', SWAP)) / 16.0  3.01 us
  transfers between devices with their start and end apart: 8, of which 4 were waited for; matrix products, arithmetic and copies ran while one was open for 1% of the time, Pallas kernels for 9%

profile of v6, /device:TPU:1, one launch (start us, length us, event | category | flops | bytes accessed | tf_op | source)
XLA Modules:
  0.0 104.3 jit_solution(3016794550090475119)
XLA Ops:
  0.6 0.9 start.1
  1.5 20.3 %all_to_all.20.own_ref = f32[32,40,128]{2,1,0:T(8,128)S(1)} all-to-all(f32[32,40,128]{2,1,0:T(8,128)S(1)} %get-tuple-element.13), channel_id=1, replica_groups=mesh['y'=4,'zl'=2,'x'=4,'c'=2,'br'=2] {'y','zl','x'}, dimensions={0} | all-to-all | bytes 1310720 | tf_op jit(solution)/shard_map/all_to_all | solution.py:261
  21.8 2.7 %collective-permute-start = (f32[32,40,128]{2,1,0:T(8,128)S(1)}, f32[32,40,128]{2,1,0:T(8,128)S(1)}, u32[]{:S(2)}, u32[]{:S(2)}) collective-permute-start(f32[32,40,128]{2,1,0:T(8,128)S(1)} %all_to_all.20.own_ref), channel_id=1, source_target_pairs={{0,2},{2,0},{1,3},{3,1},{4,6},{6,4},{5,7},{7,5},{8,10},{10,8},{9,1... | collective-permute-start | bytes 1966088 | tf_op jit(solution)/shard_map/ppermute | solution.py:262
  24.5 4.6 %own.2.e_ref = f32[16,8,512]{2,1,0:T(8,128)S(1)} custom-call(s32[1]{0:T(128)} %bitcast.par_ref, f32[32,40,128]{2,1,0:T(8,128)S(1)} %all_to_all.20.own_ref, s32[16,512]{1,0:T(8,128)S(1)} %get-tuple-element.14.idx_ref), custom_call_target="tpu_custom_call" | custom-call | tf_op jit(solution)/shard_map/own/pallas_call | solution.py:224
  29.1 0.0 collective-permute-done.oth_ref
  29.1 12.5 %main.2 = (f32[8,512]{1,0:T(8,128)S(1)}, f32[16,2,8,128]{3,2,1,0:T(8,128)}, f32[8,128]{1,0:T(8,128)S(1)}) custom-call(s32[1]{0:T(128)} %bitcast.par_ref, f32[32,40,128]{2,1,0:T(8,128)S(1)} %all_to_all.20.own_ref, f32[32,40,128]{2,1,0:T(8,128)S(1)} %collective-permute-done.oth_ref, f32[16,8,512]{2,1,0:T(8,128)S(1)} %own.2.e_ref, ...), custom_call_target="tpu_custom_call" | custom-call | tf_op jit(solution)/shard_map/main/pallas_call | solution.py:233
  41.6 3.9 %all-to-all-start.1 = ((f32[32,8,128]{2,1,0:T(8,128)}), f32[32,8,128]{2,1,0:T(8,128)S(1)}, u32[]{:S(2)}, u32[]{:S(2)}) async-start(f32[32,8,128]{2,1,0:T(8,128)} %bitcast.4), calls=%async_computation.1 | async-start | bytes 262144 | tf_op jit(solution)/shard_map/all_to_all | solution.py:284
  45.5 3.4 %collective-permute-start.1 = (f32[8,512]{1,0:T(8,128)S(1)}, f32[8,512]{1,0:T(8,128)S(1)}, u32[]{:S(2)}, u32[]{:S(2)}) collective-permute-start(f32[8,512]{1,0:T(8,128)S(1)} %get-tuple-element.17), channel_id=1, source_target_pairs={{0,1},{1,0},{2,3},{3,2},{4,5},{5,4},{6,7},{7,6},{8,9},{9,8},{10,11... | collective-permute-start | bytes 49160 | tf_op jit(solution)/shard_map/ppermute | solution.py:289
  48.9 4.2 %all-to-all-done.1 = f32[32,8,128]{2,1,0:T(8,128)S(1)} async-done(((f32[32,8,128]{2,1,0:T(8,128)}), f32[32,8,128]{2,1,0:T(8,128)S(1)}, u32[]{:S(2)}, u32[]{:S(2)}) %all-to-all-start.1) | async-done | bytes 131104 | tf_op jit(solution)/shard_map/all_to_all | solution.py:284
  53.1 1.5 %collective-permute-start.2 = (f32[8,128]{1,0:T(8,128)S(1)}, f32[8,128]{1,0:T(8,128)S(1)}, u32[]{:S(2)}, u32[]{:S(2)}) collective-permute-start(f32[8,128]{1,0:T(8,128)S(1)} %reduce_sum.18), channel_id=1, source_target_pairs={{0,2},{2,0},{1,3},{3,1},{4,6},{6,4},{5,7},{7,5},{8,10},{10,8},{9,1... | collective-permute-start | bytes 12296 | tf_op jit(solution)/shard_map/ppermute | solution.py:286
  54.6 0.0 collective-permute-done.1
  54.6 0.8 collective-permute-done.2
  55.5 14.5 %all_to_all.21.own_ref = f32[32,40,128]{2,1,0:T(8,128)S(1)} all-to-all(f32[32,40,128]{2,1,0:T(8,128)S(1)} %broadcast_in_dim.2), channel_id=1, replica_groups=mesh['y'=4,'zl'=2,'x'=4,'c'=2,'br'=2] {'y','zl','x'}, dimensions={0} | all-to-all | bytes 1310720 | tf_op jit(solution)/shard_map/all_to_all | solution.py:261
  70.0 2.7 %collective-permute-start.3 = (f32[32,40,128]{2,1,0:T(8,128)S(1)}, f32[32,40,128]{2,1,0:T(8,128)S(1)}, u32[]{:S(2)}, u32[]{:S(2)}) collective-permute-start(f32[32,40,128]{2,1,0:T(8,128)S(1)} %all_to_all.21.own_ref), channel_id=1, source_target_pairs={{0,2},{2,0},{1,3},{3,1},{4,6},{6,4},{5,7},{7,5},{8,10},{10,8},{9,1... | collective-permute-start | bytes 1966088 | tf_op jit(solution)/shard_map/ppermute | solution.py:262
  72.6 4.5 %own.3.e_ref = f32[16,8,512]{2,1,0:T(8,128)S(1)} custom-call(s32[1]{0:T(128)} %bitcast.par_ref, f32[32,40,128]{2,1,0:T(8,128)S(1)} %all_to_all.21.own_ref, s32[16,512]{1,0:T(8,128)S(1)} %get-tuple-element.14.idx_ref), custom_call_target="tpu_custom_call" | custom-call | tf_op jit(solution)/shard_map/own/pallas_call | solution.py:224
  77.2 0.0 collective-permute-done.3.oth_ref
  77.2 12.5 %main.3 = (f32[8,512]{1,0:T(8,128)S(1)}, f32[16,2,8,128]{3,2,1,0:T(8,128)}, f32[8,128]{1,0:T(8,128)}) custom-call(s32[1]{0:T(128)} %bitcast.par_ref, f32[32,40,128]{2,1,0:T(8,128)S(1)} %all_to_all.21.own_ref, f32[32,40,128]{2,1,0:T(8,128)S(1)} %collective-permute-done.3.oth_ref, f32[16,8,512]{2,1,0:T(8,128)S(1)} %own.3.e_ref, ...), custom_call_target="tpu_custom_call" | custom-call | tf_op jit(solution)/shard_map/main/pallas_call | solution.py:233
  89.7 3.9 %all-to-all-start.3 = ((f32[32,8,128]{2,1,0:T(8,128)}), f32[32,8,128]{2,1,0:T(8,128)S(1)}, u32[]{:S(2)}, u32[]{:S(2)}) async-start(f32[32,8,128]{2,1,0:T(8,128)} %bitcast.5), calls=%async_computation.3 | async-start | bytes 262144 | tf_op jit(solution)/shard_map/all_to_all | solution.py:284
  93.6 3.4 %collective-permute-start.4 = (f32[8,512]{1,0:T(8,128)S(1)}, f32[8,512]{1,0:T(8,128)S(1)}, u32[]{:S(2)}, u32[]{:S(2)}) collective-permute-start(f32[8,512]{1,0:T(8,128)S(1)} %get-tuple-element.20), channel_id=1, source_target_pairs={{0,1},{1,0},{2,3},{3,2},{4,5},{5,4},{6,7},{7,6},{8,9},{9,8},{10,11... | collective-permute-start | bytes 49160 | tf_op jit(solution)/shard_map/ppermute | solution.py:289
  97.0 4.2 %all-to-all-done.3 = f32[32,8,128]{2,1,0:T(8,128)S(1)} async-done(((f32[32,8,128]{2,1,0:T(8,128)}), f32[32,8,128]{2,1,0:T(8,128)S(1)}, u32[]{:S(2)}, u32[]{:S(2)}) %all-to-all-start.3) | async-done | bytes 131104 | tf_op jit(solution)/shard_map/all_to_all | solution.py:284
  101.3 1.5 %collective-permute-start.5 = (f32[8,128]{1,0:T(8,128)S(1)}, f32[8,128]{1,0:T(8,128)S(1)}, u32[]{:S(2)}, u32[]{:S(2)}) collective-permute-start(f32[8,128]{1,0:T(8,128)S(1)} %reduce_sum.19), channel_id=1, source_target_pairs={{0,2},{2,0},{1,3},{3,1},{4,6},{6,4},{5,7},{7,5},{8,10},{10,8},{9,1... | collective-permute-start | bytes 12296 | tf_op jit(solution)/shard_map/ppermute | solution.py:286
  102.8 0.0 collective-permute-done.4
  102.8 0.6 add.34
  103.4 0.2 collective-permute-done.5
  103.6 0.7 slice_select_fusion
  (7 shorter events, 0.1 us)
Async XLA Ops:
  21.8 7.3 %collective-permute-start = (f32[32,40,128]{2,1,0:T(8,128)S(1)}, f32[32,40,128]{2,1,0:T(8,128)S(1)}, u32[]{:S(2)}, u32[]{:S(2)}) collective-permute-start(f32[32,40,128]{2,1,0:T(8,128)S(1)} %all_to_all.20.own_ref), channel_id=1, source_target_pairs={{0,2},{2,0},{1,3},{3,1},{4,6},{6,4},{5,7},{7,5},{8,10},{10,8},{9,1... | collective-permute-start | bytes 1966088 | tf_op jit(solution)/shard_map/ppermute | solution.py:262
  41.6 11.5 %all-to-all-start.1 = ((f32[32,8,128]{2,1,0:T(8,128)}), f32[32,8,128]{2,1,0:T(8,128)S(1)}, u32[]{:S(2)}, u32[]{:S(2)}) async-start(f32[32,8,128]{2,1,0:T(8,128)} %bitcast.4), calls=%async_computation.1 | async-start | bytes 262144 | tf_op jit(solution)/shard_map/all_to_all | solution.py:284
  45.5 9.1 %collective-permute-start.1 = (f32[8,512]{1,0:T(8,128)S(1)}, f32[8,512]{1,0:T(8,128)S(1)}, u32[]{:S(2)}, u32[]{:S(2)}) collective-permute-start(f32[8,512]{1,0:T(8,128)S(1)} %get-tuple-element.17), channel_id=1, source_target_pairs={{0,1},{1,0},{2,3},{3,2},{4,5},{5,4},{6,7},{7,6},{8,9},{9,8},{10,11... | collective-permute-start | bytes 49160 | tf_op jit(solution)/shard_map/ppermute | solution.py:289
  53.1 2.3 %collective-permute-start.2 = (f32[8,128]{1,0:T(8,128)S(1)}, f32[8,128]{1,0:T(8,128)S(1)}, u32[]{:S(2)}, u32[]{:S(2)}) collective-permute-start(f32[8,128]{1,0:T(8,128)S(1)} %reduce_sum.18), channel_id=1, source_target_pairs={{0,2},{2,0},{1,3},{3,1},{4,6},{6,4},{5,7},{7,5},{8,10},{10,8},{9,1... | collective-permute-start | bytes 12296 | tf_op jit(solution)/shard_map/ppermute | solution.py:286
  70.0 7.2 %collective-permute-start.3 = (f32[32,40,128]{2,1,0:T(8,128)S(1)}, f32[32,40,128]{2,1,0:T(8,128)S(1)}, u32[]{:S(2)}, u32[]{:S(2)}) collective-permute-start(f32[32,40,128]{2,1,0:T(8,128)S(1)} %all_to_all.21.own_ref), channel_id=1, source_target_pairs={{0,2},{2,0},{1,3},{3,1},{4,6},{6,4},{5,7},{7,5},{8,10},{10,8},{9,1... | collective-permute-start | bytes 1966088 | tf_op jit(solution)/shard_map/ppermute | solution.py:262
  89.7 11.5 %all-to-all-start.3 = ((f32[32,8,128]{2,1,0:T(8,128)}), f32[32,8,128]{2,1,0:T(8,128)S(1)}, u32[]{:S(2)}, u32[]{:S(2)}) async-start(f32[32,8,128]{2,1,0:T(8,128)} %bitcast.5), calls=%async_computation.3 | async-start | bytes 262144 | tf_op jit(solution)/shard_map/all_to_all | solution.py:284
  93.6 9.1 %collective-permute-start.4 = (f32[8,512]{1,0:T(8,128)S(1)}, f32[8,512]{1,0:T(8,128)S(1)}, u32[]{:S(2)}, u32[]{:S(2)}) collective-permute-start(f32[8,512]{1,0:T(8,128)S(1)} %get-tuple-element.20), channel_id=1, source_target_pairs={{0,1},{1,0},{2,3},{3,2},{4,5},{5,4},{6,7},{7,6},{8,9},{9,8},{10,11... | collective-permute-start | bytes 49160 | tf_op jit(solution)/shard_map/ppermute | solution.py:289
  101.3 2.3 %collective-permute-start.5 = (f32[8,128]{1,0:T(8,128)S(1)}, f32[8,128]{1,0:T(8,128)S(1)}, u32[]{:S(2)}, u32[]{:S(2)}) collective-permute-start(f32[8,128]{1,0:T(8,128)S(1)} %reduce_sum.19), channel_id=1, source_target_pairs={{0,2},{2,0},{1,3},{3,1},{4,6},{6,4},{5,7},{7,5},{8,10},{10,8},{9,1... | collective-permute-start | bytes 12296 | tf_op jit(solution)/shard_map/ppermute | solution.py:286
